TPU v7x, 256 devices: a whole 4x4x8 slice. The times are simulated.
256 devices in a mesh: rep: 32 (over x, z), tp: 8 (over y, core).
Axes of the slice: x: 4, y: 4, z: 8, core: 2. Of those that a mesh axis runs over, the one named last changes fastest.
Arguments:
- hidden: bfloat16 [256, 2, 8192], P('rep'), may hold values from -6 to 6
- queries: bfloat16 [256, 2, 8192], P('rep', None, 'tp')
- key_weight: bfloat16 [8192, 1024], P(None, 'tp'), may hold values from -0.0625 to 0.0625
- value_weight: bfloat16 [8192, 1024], P(None, 'tp'), may hold values from -0.0625 to 0.0625
- adapter_down_weight: bfloat16 [512, 8192, 64], P('rep', 'tp'), may hold values from -0.0625 to 0.0625
- adapter_up_weight: bfloat16 [512, 64, 1024], P('rep', None, 'tp'), may hold values from -0.75 to 0.75
- row_adapter_index: int32 [256], P('rep'), may hold values from 0 to 511, as said below
- adapter_home_slot: int32 [512], replicated, may hold values from 0 to 511, as said below
- row_page_table: int32 [256, 8], P('rep'), may hold values from 0 to 63, as said below
- lengths: int32 [32, 8], P('rep'), may hold values from 1 to 1024, 5120 in all within a row
- row_serving_slot: int32 [256], P('rep'), may hold values from 0 to 511, as said below
- paged_key_cache: bfloat16 [2048, 128, 1024], P('rep', None, 'tp'), may hold values from -6 to 6
- paged_value_cache: bfloat16 [2048, 128, 1024], P('rep', None, 'tp'), may hold values from -6 to 6
Outputs:
- attended: bfloat16 [512, 2, 8192], P('rep', None, 'tp')
Inputs may be any that keep to these rules, and one draw needn't show every extreme that they name: `row_adapter_index`: adapter a's maps are adapter_down_weight[adapter_home_slot[a]] and adapter_up_weight[adapter_home_slot[a]]; the rows of one replica use adapters with distinct home slots // 16. `adapter_home_slot`: A permutation. `row_page_table`: the rows of one replica use distinct pages of its pool. `lengths`: each sequence holds at most 1024 positions; the 8 sequences of one replica (one line of the array) together hold 5120 positions. `row_serving_slot`: slots are distinct. A quarter of the replicas are preempted: their rows name slots 8 to 15 of other replicas, at most 2 rows of one replica in one other replica; every other replica keeps row i of its own in its slot i.
All inputs are finite; a program needn't handle non-finite values.
Results may differ from a plain program's by a relative error of at most 0.0051.
Values may be sent and summed in bfloat16 or wider, within the bound.
A program may use at most 64 MiB of HBM per device.

v0:
```python
import jax
import jax.numpy as jnp
from jax import lax
from jax.sharding import PartitionSpec as P

HEAD_SIZE = 128


rope_base = 1000000.0
adapter_scale = 0.5


def sent_to_all(value, axis):
    size = lax.axis_size(axis)
    return lax.all_to_all(
        jnp.broadcast_to(value[None], (size, *value.shape)), axis, 0, 0, tiled=True
    )


def taken_together(value, axis):
    return sent_to_all(value, axis).sum(axis=0)


def rotate(keys, positions, width):
    half = width // 2
    freqs = rope_base ** (-2.0 * jnp.arange(half, dtype=jnp.float32) / width)
    angles = positions[..., None] * freqs
    first = keys[..., :half]
    second = keys[..., half:]
    cosine = jnp.cos(angles)
    sine = jnp.sin(angles)
    return jnp.concatenate(
        [first * cosine - second * sine, second * cosine + first * sine], axis=-1
    )


def shards(
    hidden,
    queries,
    key_weight,
    value_weight,
    adapter_down_weight,
    adapter_up_weight,
    row_adapter_index,
    adapter_home_slot,
    row_page_table,
    lengths,
    row_serving_slot,
    paged_key_cache,
    paged_value_cache,
):
    rows = hidden.shape[0]
    width = hidden.shape[2]
    head_dim = HEAD_SIZE
    kv_local = key_weight.shape[1] // head_dim
    group = queries.shape[2] // (kv_local * head_dim)
    slice_column_width = adapter_down_weight.shape[1]
    adapters_per_replica = adapter_down_weight.shape[0]
    n_rep = lax.axis_size("rep")
    rep_index = lax.axis_index("rep")
    tp_index = lax.axis_index("tp")
    cached_len = lengths.reshape(-1)
    flat = hidden.reshape(rows * 2, width)
    new_keys = jnp.dot(flat, key_weight, preferred_element_type=jnp.float32).reshape(
        rows, 2, kv_local, head_dim
    )
    positions = (cached_len[:, None] + jnp.arange(2, dtype=jnp.int32)[None, :]).astype(jnp.float32)
    new_keys = rotate(new_keys, positions[:, :, None], head_dim).astype(jnp.bfloat16)
    plain_values = jnp.dot(flat, value_weight, preferred_element_type=jnp.float32).reshape(
        rows, 2, kv_local * head_dim
    )
    home_slot = adapter_home_slot[row_adapter_index]
    owner = home_slot // adapters_per_replica
    within = home_slot % adapters_per_replica
    rows_slice = lax.dynamic_slice_in_dim(
        hidden, tp_index * slice_column_width, slice_column_width, 2
    )
    send_rows = (
        jnp.zeros((n_rep, 1, 2, slice_column_width), jnp.bfloat16).at[owner, 0].set(rows_slice)
    )
    send_within = jnp.full((n_rep, 1), -1, jnp.int32).at[owner, 0].set(within)
    arrived = lax.all_to_all(send_rows, "rep", split_axis=0, concat_axis=0, tiled=True)
    chosen = lax.all_to_all(send_within, "rep", split_axis=0, concat_axis=0, tiled=True)
    valid = chosen >= 0
    safe = jnp.maximum(chosen, 0)
    partial_value = jnp.einsum(
        "sntd,sndr->sntr", arrived, adapter_down_weight[safe], preferred_element_type=jnp.float32
    )
    summed = taken_together(partial_value, "tp").astype(jnp.bfloat16)
    single_term = jnp.einsum(
        "sntr,snrc->sntc", summed, adapter_up_weight[safe], preferred_element_type=jnp.float32
    )
    terms = jnp.where(valid[:, :, None, None], single_term, 0.0)
    returned = lax.all_to_all(terms, "rep", split_axis=0, concat_axis=0, tiled=True)
    adapter_value_terms = returned[owner, 0]
    fresh_values = (
        (plain_values + adapter_scale * adapter_value_terms)
        .astype(jnp.bfloat16)
        .reshape(rows, 2, kv_local, head_dim)
    )
    page_keys = paged_key_cache[row_page_table].reshape(rows, -1, kv_local, head_dim)
    page_values = paged_value_cache[row_page_table].reshape(rows, -1, kv_local, head_dim)
    span = page_keys.shape[1]
    query_heads = queries.reshape(rows, 2, kv_local, group, head_dim)
    scale = head_dim ** (-0.5)
    old_scores = (
        jnp.einsum("rtkgd,rjkd->rtkgj", query_heads, page_keys, preferred_element_type=jnp.float32)
        * scale
    )
    seen = jnp.arange(span)[None, :] < cached_len[:, None]
    old_scores = jnp.where(seen[:, None, None, None, :], old_scores, -jnp.inf)
    new_scores = (
        jnp.einsum("rtkgd,rskd->rtkgs", query_heads, new_keys, preferred_element_type=jnp.float32)
        * scale
    )
    causal = jnp.arange(2)[None, :] <= jnp.arange(2)[:, None]
    new_scores = jnp.where(causal[None, :, None, None, :], new_scores, -jnp.inf)
    peak = jnp.maximum(old_scores.max(-1), new_scores.max(-1))[..., None]
    old_exp = jnp.exp(old_scores - peak)
    new_exp = jnp.exp(new_scores - peak)
    total = (old_exp.sum(-1) + new_exp.sum(-1))[..., None]
    old_weights = (old_exp / total).astype(jnp.bfloat16)
    new_weights = (new_exp / total).astype(jnp.bfloat16)
    mixed = jnp.einsum(
        "rtkgj,rjkd->rtkgd", old_weights, page_values, preferred_element_type=jnp.float32
    )
    mixed = mixed + jnp.einsum(
        "rtkgs,rskd->rtkgd", new_weights, fresh_values, preferred_element_type=jnp.float32
    )
    served = mixed.astype(jnp.bfloat16).reshape(rows, 2, kv_local * group * head_dim)
    columns = served.shape[2]
    slots = 2 * rows
    target = row_serving_slot // slots
    quarter = n_rep // 4
    most = 2 * ((rows // 2 + quarter - 1) // quarter)
    away = target != rep_index
    earlier = jnp.arange(rows)[None, :] < jnp.arange(rows)[:, None]
    same = (target[:, None] == target[None, :]) & earlier
    order_rank = jnp.sum(same.astype(jnp.int32), axis=1)
    destination = jnp.where(away, target, n_rep)
    send_out = (
        jnp.zeros((n_rep, most, 2, columns), jnp.bfloat16)
        .at[destination, order_rank]
        .set(served, mode="drop")
    )
    send_slot = (
        jnp.full((n_rep, most), slots, jnp.int32)
        .at[destination, order_rank]
        .set(row_serving_slot - target * slots, mode="drop")
    )
    got_out, got_slot = (
        lax.all_to_all(send_out, "rep", split_axis=0, concat_axis=0, tiled=True),
        lax.all_to_all(send_slot, "rep", split_axis=0, concat_axis=0, tiled=True),
    )
    kept_slot = jnp.where(away, slots, row_serving_slot - rep_index * slots)
    values_all = jnp.concatenate([served, got_out.reshape(-1, 2, columns)], axis=0)
    slot_all = jnp.concatenate([kept_slot, got_slot.reshape(-1)], axis=0)
    result = jnp.zeros((slots, 2, columns), jnp.bfloat16).at[slot_all].set(values_all, mode="drop")
    return result


def solution(mesh):
    placed = (
        P("rep", None, None),
        P("rep", None, "tp"),
        P(None, "tp"),
        P(None, "tp"),
        P("rep", "tp", None),
        P("rep", None, "tp"),
        P("rep"),
        P(),
        P("rep", None),
        P("rep", None),
        P("rep"),
        P("rep", None, "tp"),
        P("rep", None, "tp"),
    )
    return jax.shard_map(
        shards, mesh=mesh, in_specs=placed, out_specs=P("rep", None, "tp"), check_vma=False
    )
```

profile of v0, /device:TPU:8, one launch (start us, length us, event | category | flops | bytes accessed | tf_op | source)
XLA Modules:
  0.0 127.5 jit_solution(4654984507441097889)
XLA Ops:
  0.0 0.0 copy-start
  0.0 0.8 compare_select_fusion.2
  0.8 1.3 %gather_fusion.2 = s32[8]{0:T(128)S(1)} fusion(s32[512]{0:T(512)} %param.20, s32[1024]{0:T(1024)S(1)} %pad_clamp_fusion.1), kind=kCustom, calls=%fused_computation.2 | custom fusion | bytes 96 | tf_op jit(solution)/shard_map/gather | solution.py:72
  2.2 0.6 scatter_custom_fusion.1
  2.8 0.7 copy.41
  3.5 11.3 %all-to-all-start.1 = ((s32[32,1,1]{2,1,0:T(1,128)}), s32[32,1,1]{2,1,0:T(1,128)S(1)}, u32[]{:S(2)}, u32[]{:S(2)}) async-start(s32[32,1,1]{2,1,0:T(1,128)} %copy.41), calls=%async_computation.1 | async-start | bytes 32768 | tf_op jit(solution)/shard_map/all_to_all | solution.py:83
  14.8 0.7 add_convert_fusion
  15.5 0.7 iota_compare_fusion
  16.2 0.8 reshape.382
  17.0 0.7 compare_select_fusion
  17.7 0.1 reshape.392
  17.8 2.1 %fusion.11 = f32[8,2,1,128]{3,0,1,2:T(8,128)S(1)} fusion(bf16[8192,128]{1,0:T(8,128)(2,1)} %param.15, bf16[8,2,8192]{2,1,0:T(2,128)(2,1)} %param.13), kind=kOutput, calls=%fused_computation.26 | convolution fusion | flops 33554432 | bytes 2367488 | tf_op jit(solution)/shard_map/dot_general | solution.py:64
  19.9 0.1 fusion.47
  20.1 0.1 maximum_bitcast_fusion
  20.2 3.8 %gather_fusion.1 = bf16[64,128,128]{2,1,0:T(8,128)(2,1)} fusion(bf16[64,128,128]{2,1,0:T(8,128)(2,1)} %param.24, s32[1024]{0:T(1024)S(1)} %pad_clamp_fusion.2), kind=kCustom, calls=%fused_computation.1 | custom fusion | bytes 4194560 | tf_op jit(solution)/shard_map/gather | solution.py:101
  23.9 0.3 fusion.59
  24.2 2.3 %fusion.58 = (f32[8,2,8]{2,1,0:T(2,128)S(1)}, f32[8,2,1,8,1024]{4,3,1,0,2:T(8,128)S(1)}) fusion(bf16[8,1024,128,1]{2,1,3,0:T(8,128)(2,1)} %bitcast.121, bf16[8,2,8,128]{3,2,1,0:T(8,128)(2,1)S(1)} %reshape.382, pred[8,1024]{1,0:T(8,128)(4,1)S(1)} %iota_compare_fusion), kind=kOutput, calls=%fused_computation.111 | convolution fusion | flops 33947520 | bytes 2662912 | tf_op jit(solution)/shard_map/rtkgd,rjkd->rtkgj/dot_general | solution.py:107
  26.6 0.2 fusion.24
  26.8 3.8 %gather_fusion = bf16[64,128,128]{2,1,0:T(8,128)(2,1)} fusion(bf16[64,128,128]{2,1,0:T(8,128)(2,1)} %param.25, s32[1024]{0:T(1024)S(1)} %pad_clamp_fusion.2), kind=kCustom, calls=%fused_computation | custom fusion | bytes 4194560 | tf_op jit(solution)/shard_map/gather | solution.py:102
  30.6 0.0 copy-start.1
  30.6 2.1 %fusion.25 = f32[8,128,2,8]{1,3,2,0:T(8,128)S(1)} fusion(bf16[8,1024,128,1]{2,1,3,0:T(8,128)(2,1)} %bitcast.122, f32[8,2,1,8,1024]{4,3,1,0,2:T(8,128)S(1)} %get-tuple-element.12, f32[8,2,8]{2,1,0:T(2,128)S(1)} %add.115, f32[8,2,8]{2,1,0:T(2,128)S(1)} %max.15), kind=kOutput, calls=%fused_computation.35 | convolution fusion | flops 33947648 | bytes 2688000 | tf_op jit(solution)/shard_map/rtkgj,rjkd->rtkgd/dot_general | solution.py:124
  32.7 0.0 copy-done.3
  32.7 0.0 copy-done.1
  32.8 0.7 broadcast.289
  33.5 2.0 %scatter_fusion.1 = bf16[32,2,1024]{2,1,0:T(2,128)(2,1)} fusion(bf16[32,2,1024]{2,1,0:T(2,128)(2,1)} %broadcast.289, s32[8]{0:T(128)S(1)} %get-tuple-element.10, bf16[8,2,1024]{2,1,0:T(2,128)(2,1)S(1)} %constant_dynamic-slice_fusion), kind=kCustom, calls=%fused_computation.8 | custom fusion | bytes 98336 | tf_op jit(solution)/shard_map/scatter | solution.py:79
  35.5 0.0 all-to-all-done.1
  35.5 9.8 %all-to-all-start.2 = ((bf16[32,1,2,1024]{3,2,1,0:T(2,128)(2,1)}), bf16[32,1,2,1024]{3,2,1,0:T(2,128)(2,1)S(1)}, u32[]{:S(2)}, u32[]{:S(2)}) async-start(bf16[32,1,2,1024]{3,2,1,0:T(2,128)(2,1)} %bitcast.28), calls=%async_computation.2 | async-start | bytes 262144 | tf_op jit(solution)/shard_map/all_to_all | solution.py:82
  45.3 0.7 maximum_reduce_fusion
  46.0 0.0 copy-done
  46.0 2.7 %gather_fusion.3 = bf16[32,1024,64]{1,2,0:T(8,128)(2,1)} fusion(bf16[16,1024,64]{1,2,0:T(8,128)(2,1)S(1)} %copy-done, s32[1024]{0:T(1024)S(1)} %pad_clamp_fusion), kind=kCustom, calls=%fused_computation.3 | custom fusion | bytes 8388736 | tf_op jit(solution)/shard_map/gather | solution.py:87
  48.7 0.0 copy-start.2
  48.7 7.0 %all-to-all-done.2 = bf16[32,1,2,1024]{3,2,1,0:T(2,128)(2,1)S(1)} async-done(((bf16[32,1,2,1024]{3,2,1,0:T(2,128)(2,1)}), bf16[32,1,2,1024]{3,2,1,0:T(2,128)(2,1)S(1)}, u32[]{:S(2)}, u32[]{:S(2)}) %all-to-all-start.2) | async-done | bytes 131104 | tf_op jit(solution)/shard_map/all_to_all | solution.py:82
  55.7 3.4 %fusion.30 = f32[32,2,64]{2,1,0:T(2,128)S(1)} fusion(bf16[32,1024,64]{1,2,0:T(8,128)(2,1)} %gather_fusion.3, bf16[32,1,2,1024]{3,2,1,0:T(2,128)(2,1)S(1)} %all-to-all-done.2), kind=kOutput, calls=%fused_computation.40 | convolution fusion | flops 8388608 | bytes 4341760 | tf_op jit(solution)/shard_map/sntd,sndr->sntr/dot_general | solution.py:86
  59.1 0.8 reshape.505
  60.0 4.9 %all-to-all-start.3 = ((f32[8,1,4096]{2,1,0:T(1,128)}), f32[8,1,4096]{2,1,0:T(1,128)S(1)}, u32[]{:S(2)}, u32[]{:S(2)}) async-start(f32[8,1,4096]{2,1,0:T(1,128)} %reshape.505), calls=%async_computation.3 | async-start | bytes 262144 | tf_op jit(solution)/shard_map/all_to_all | solution.py:15
  64.9 0.2 convert_reduce_fusion
  65.1 0.0 copy-done.2
  65.1 0.6 gather_fusion.4
  65.7 0.7 compare_reduce_fusion
  66.4 3.1 %all-to-all-done.3 = f32[8,1,4096]{2,1,0:T(1,128)S(1)} async-done(((f32[8,1,4096]{2,1,0:T(1,128)}), f32[8,1,4096]{2,1,0:T(1,128)S(1)}, u32[]{:S(2)}, u32[]{:S(2)}) %all-to-all-start.3) | async-done | bytes 131104 | tf_op jit(solution)/shard_map/all_to_all | solution.py:15
  69.5 0.5 broadcast.355
  70.0 1.0 reduce.13
  71.0 0.1 reshape.506
  71.1 0.9 fusion.9
  72.0 3.9 %all-to-all-start.4 = ((f32[32,1,2,128]{3,2,1,0:T(2,128)}), f32[32,1,2,128]{3,2,1,0:T(2,128)S(1)}, u32[]{:S(2)}, u32[]{:S(2)}) async-start(f32[32,1,2,128]{3,2,1,0:T(2,128)} %fusion.9), calls=%async_computation.4 | async-start | bytes 65536 | tf_op jit(solution)/shard_map/all_to_all | solution.py:94
  75.9 0.8 scatter_fusion
  76.7 0.7 copy.37
  77.4 8.3 %all-to-all-done.4 = f32[32,1,2,128]{3,2,1,0:T(2,128)S(1)} async-done(((f32[32,1,2,128]{3,2,1,0:T(2,128)}), f32[32,1,2,128]{3,2,1,0:T(2,128)S(1)}, u32[]{:S(2)}, u32[]{:S(2)}) %all-to-all-start.4) | async-done | bytes 32800 | tf_op jit(solution)/shard_map/all_to_all | solution.py:94
  85.7 3.8 %all-to-all-start = ((s32[32,1,2]{2,1,0:T(1,128)}), s32[32,1,2]{2,1,0:T(1,128)S(1)}, u32[]{:S(2)}, u32[]{:S(2)}) async-start(s32[32,1,2]{2,1,0:T(1,128)} %copy.37), calls=%async_computation | async-start | bytes 32768 | tf_op jit(solution)/shard_map/all_to_all | solution.py:153
  89.5 0.6 gather_fusion.5
  90.1 2.1 %fusion.20 = bf16[8,2,128,1]{2,0,1,3:T(8,128)(2,1)S(1)} fusion(bf16[8192,128]{1,0:T(8,128)(2,1)} %param.16, bf16[8,2,8192]{2,1,0:T(2,128)(2,1)S(1)} %copy-done.1, f32[8,2,128]{2,1,0:T(2,128)S(1)} %gather_fusion.5), kind=kOutput, calls=%fused_computation.29 | convolution fusion | flops 33560576 | bytes 2371584 | tf_op jit(solution)/shard_map/dot_general | solution.py:69
  92.2 0.2 fusion.8
  92.4 0.8 broadcast_in_dim.114
  93.3 1.7 %scatter_fusion.2 = bf16[32,2,2,1024]{3,2,1,0:T(2,128)(2,1)} fusion(bf16[32,2,2,1024]{3,2,1,0:T(2,128)(2,1)} %broadcast_in_dim.114, s32[8]{0:T(128)S(1)} %fusion.54, bf16[8,2,1024]{2,1,0:T(2,128)(2,1)S(1)} %reshape.464), kind=kCustom, calls=%fused_computation.9 | custom fusion | bytes 98368 | tf_op jit(solution)/shard_map/scatter | solution.py:144
  95.0 4.3 %all-to-all-done = s32[32,1,2]{2,1,0:T(1,128)S(1)} async-done(((s32[32,1,2]{2,1,0:T(1,128)}), s32[32,1,2]{2,1,0:T(1,128)S(1)}, u32[]{:S(2)}, u32[]{:S(2)}) %all-to-all-start) | async-done | bytes 288 | tf_op jit(solution)/shard_map/all_to_all | solution.py:153
  99.4 5.5 %all-to-all-start.5 = ((bf16[32,2,2,1024]{3,2,1,0:T(2,128)(2,1)}), bf16[32,2,2,1024]{3,2,1,0:T(2,128)(2,1)S(1)}, u32[]{:S(2)}, u32[]{:S(2)}) async-start(bf16[32,2,2,1024]{3,2,1,0:T(2,128)(2,1)} %scatter_fusion.2), calls=%async_computation.5 | async-start | bytes 524288 | tf_op jit(solution)/shard_map/all_to_all | solution.py:152
  104.8 0.5 broadcast.353
  105.3 0.7 reduce.12
  106.0 0.1 concatenate.51
  106.1 0.1 fusion.53
  106.2 10.2 %all-to-all-done.5 = bf16[32,2,2,1024]{3,2,1,0:T(2,128)(2,1)S(1)} async-done(((bf16[32,2,2,1024]{3,2,1,0:T(2,128)(2,1)}), bf16[32,2,2,1024]{3,2,1,0:T(2,128)(2,1)S(1)}, u32[]{:S(2)}, u32[]{:S(2)}) %all-to-all-start.5) | async-done | bytes 262176 | tf_op jit(solution)/shard_map/all_to_all | solution.py:152
  116.4 0.4 pad_maximum_fusion
  116.8 0.7 broadcast_in_dim.61
  117.5 10.0 %scatter_fusion.3 = bf16[16,2,1024]{2,1,0:T(2,128)(2,1)} fusion(bf16[16,2,1024]{2,1,0:T(2,128)(2,1)} %broadcast_in_dim.61, s32[72]{0:T(128)S(1)} %fusion.53, bf16[72,2,1024]{2,1,0:T(2,128)(2,1)S(1)} %pad_maximum_fusion), kind=kCustom, calls=%fused_computation.10 | custom fusion | bytes 885024 | tf_op jit(solution)/shard_map/scatter | solution.py:158
  (20 shorter events, 0.3 us)
Async XLA Ops:
  0.0 46.0 %copy-start = (bf16[16,1024,64]{1,2,0:T(8,128)(2,1)S(1)}, bf16[16,1024,64]{1,2,0:T(8,128)(2,1)}, u32[]{:S(2)}) copy-start(bf16[16,1024,64]{1,2,0:T(8,128)(2,1)} %param.17) | copy-start | bytes 6291460
  3.5 32.0 %all-to-all-start.1 = ((s32[32,1,1]{2,1,0:T(1,128)}), s32[32,1,1]{2,1,0:T(1,128)S(1)}, u32[]{:S(2)}, u32[]{:S(2)}) async-start(s32[32,1,1]{2,1,0:T(1,128)} %copy.41), calls=%async_computation.1 | async-start | bytes 32768 | tf_op jit(solution)/shard_map/all_to_all | solution.py:83
  30.6 2.1 %copy-start.3 = (s32[8]{0:T(128)S(1)}, s32[8]{0:T(128)}, u32[]{:S(2)}) copy-start(s32[8]{0:T(128)} %param.23) | copy-start | bytes 100
  30.6 2.1 %copy-start.1 = (bf16[8,2,8192]{2,1,0:T(2,128)(2,1)S(1)}, bf16[8,2,8192]{2,1,0:T(2,128)(2,1)}, u32[]{:S(2)}) copy-start(bf16[8,2,8192]{2,1,0:T(2,128)(2,1)} %param.13) | copy-start | bytes 786436
  35.5 20.2 %all-to-all-start.2 = ((bf16[32,1,2,1024]{3,2,1,0:T(2,128)(2,1)}), bf16[32,1,2,1024]{3,2,1,0:T(2,128)(2,1)S(1)}, u32[]{:S(2)}, u32[]{:S(2)}) async-start(bf16[32,1,2,1024]{3,2,1,0:T(2,128)(2,1)} %bitcast.28), calls=%async_computation.2 | async-start | bytes 262144 | tf_op jit(solution)/shard_map/all_to_all | solution.py:82
  48.7 16.4 %copy-start.2 = (bf16[16,64,128]{2,1,0:T(8,128)(2,1)S(1)}, bf16[16,64,128]{2,1,0:T(8,128)(2,1)}, u32[]{:S(2)}) copy-start(bf16[16,64,128]{2,1,0:T(8,128)(2,1)} %param.18) | copy-start | bytes 786436
  60.0 9.6 %all-to-all-start.3 = ((f32[8,1,4096]{2,1,0:T(1,128)}), f32[8,1,4096]{2,1,0:T(1,128)S(1)}, u32[]{:S(2)}, u32[]{:S(2)}) async-start(f32[8,1,4096]{2,1,0:T(1,128)} %reshape.505), calls=%async_computation.3 | async-start | bytes 262144 | tf_op jit(solution)/shard_map/all_to_all | solution.py:15
  72.0 13.7 %all-to-all-start.4 = ((f32[32,1,2,128]{3,2,1,0:T(2,128)}), f32[32,1,2,128]{3,2,1,0:T(2,128)S(1)}, u32[]{:S(2)}, u32[]{:S(2)}) async-start(f32[32,1,2,128]{3,2,1,0:T(2,128)} %fusion.9), calls=%async_computation.4 | async-start | bytes 65536 | tf_op jit(solution)/shard_map/all_to_all | solution.py:94
  85.7 13.7 %all-to-all-start = ((s32[32,1,2]{2,1,0:T(1,128)}), s32[32,1,2]{2,1,0:T(1,128)S(1)}, u32[]{:S(2)}, u32[]{:S(2)}) async-start(s32[32,1,2]{2,1,0:T(1,128)} %copy.37), calls=%async_computation | async-start | bytes 32768 | tf_op jit(solution)/shard_map/all_to_all | solution.py:153
  99.4 17.1 %all-to-all-start.5 = ((bf16[32,2,2,1024]{3,2,1,0:T(2,128)(2,1)}), bf16[32,2,2,1024]{3,2,1,0:T(2,128)(2,1)S(1)}, u32[]{:S(2)}, u32[]{:S(2)}) async-start(bf16[32,2,2,1024]{3,2,1,0:T(2,128)(2,1)} %scatter_fusion.2), calls=%async_computation.5 | async-start | bytes 524288 | tf_op jit(solution)/shard_map/all_to_all | solution.py:152
where the time goes:
time: 129 us; the launch traced here: 127 us
  starting transfers between devices  39.1 us (30%)
  local copies, waits for them, and re-layouts  34.6 us (27%)
  waiting for transfers between devices  33 us (26%)
  matrix products  13.4 us (10%)
  other arithmetic  7.11 us (6%)
    all_to_all x1, starting transfers between devices, shards(): lax.all_to_all(send_within, 'rep', split_axis=0, concat_axis=0, tiled=True)  11.3 us
    all_to_all x1, waiting for transfers between devices, shards(): lax.all_to_all(send_out, 'rep', split_axis=0, concat_axis=0, tiled=True)  10.2 us
    scatter x1, local copies, waits for them, and re-layouts, shards(): jnp.zeros((slots, 2, columns), jnp.bfloat16).at[slot_all]  9.98 us
    all_to_all x1, starting transfers between devices, shards(): lax.all_to_all(send_rows, 'rep', split_axis=0, concat_axis=0, tiled=True)  9.77 us
    all_to_all x1, waiting for transfers between devices, shards(): lax.all_to_all(terms, 'rep', split_axis=0, concat_axis=0, tiled=True)  8.29 us
    all_to_all x1, waiting for transfers between devices, shards(): lax.all_to_all(send_rows, 'rep', split_axis=0, concat_axis=0, tiled=True)  7.01 us
    all_to_all x1, starting transfers between devices, shards(): lax.all_to_all(send_out, 'rep', split_axis=0, concat_axis=0, tiled=True)  5.46 us
    all_to_all x1, starting transfers between devices, sent_to_all(): lax.all_to_all(jnp.broadcast_to(value[None], (size, *value.shape)), axis,...  4.92 us
  transfers between devices with their start and end apart: 6, of which 5 were waited for; matrix products, arithmetic and copies ran while one was open for 27% of the time, Pallas kernels for 0%

commit v1 on v0

v1 whole, which is shorter than its diff:
```python
import functools
import math

import jax
import jax.numpy as jnp
from jax import lax
from jax.experimental import pallas as pl
from jax.experimental.pallas import tpu as pltpu
from jax.sharding import PartitionSpec as P

MESH = pl.DeviceIdType.MESH
F32, BF16, I32 = jnp.float32, jnp.bfloat16, jnp.int32

NX, NZ, TP = 4, 8, 8
NREP = NX * NZ
ROWS, SLOTS, ADP, RANK = 8, 16, 16, 64
LANES = 128
CHUNKS = 64
NT = (((1,), (1,)), ((), ()))
LOG_BASE = math.log(1000000.0)


def kernel(
    hid, qin, wk, wv, dn, up, ridx, home, table, length, serve, kc, vc,
    out,
    hidv, qv, wkv, wvv, dnv, upv, kv, vv, ridx_s, home_s, table_s, length_s, serve_s,
    hf, xl, sb, arr, af, xs, mb, mrec, tb, trec, cs, crec, mixed, wn0s, wn1s, nkf, pvs, served, sb4, grec,
    idx_s, code_s, in_sem, send_sem, recv_sem,
):
    me = lax.axis_index("rep")
    tp = lax.axis_index("tp")
    mx, mz = me // NZ, me % NZ

    def far(a):
        return ((mx + 2 + a % NX) % NX) * NZ + (mz + 4 + a // NX) % NZ

    def peers(do):
        def step(a, carry):
            do(far(a))
            return carry

        lax.fori_loop(0, 18, step, 0)
        lax.fori_loop(19, 32, step, 0)

    def tp_peers(do):
        def step(a, carry):
            do((tp + a) % TP)
            return carry

        lax.fori_loop(1, TP, step, 0)

    bar = pltpu.get_barrier_semaphore()
    peers(lambda d: pl.semaphore_signal(bar, inc=1, device_id=(d, tp), device_id_type=MESH))
    tp_peers(lambda d: pl.semaphore_signal(bar, inc=1, device_id=(me, d), device_id_type=MESH))

    pairs = [
        (ridx, ridx_s), (home, home_s), (serve, serve_s), (hid, hidv), (length, length_s), (table, table_s),
        (wk, wkv), (qin, qv), (kc, kv), (vc, vv), (wv, wvv), (dn, dnv), (up, upv),
    ]
    loads = [pltpu.make_async_copy(s, d, in_sem.at[n]) for n, (s, d) in enumerate(pairs)]
    for c in loads:
        c.start()
    (l_ridx, l_home, l_serve, l_hid, l_len, l_tab, l_wk, l_q, l_k, l_v, l_wv, l_dn, l_up) = loads

    l_ridx.wait()
    l_home.wait()
    l_serve.wait()
    homes = [home_s[ridx_s[i]] for i in range(ROWS)]
    owners = [h // ADP for h in homes]
    slots = [serve_s[i] for i in range(ROWS)]
    lane1 = lax.broadcasted_iota(I32, (1, LANES), 1)
    meta = jnp.zeros((1, LANES), I32)
    for i in range(ROWS):
        meta = jnp.where(lane1 == i, homes[i], meta)
        meta = jnp.where(lane1 == ROWS + i, slots[i], meta)
    mb[...] = meta
    l_hid.wait()
    mine = pl.multiple_of(tp * 16, 16)

    def fill(d, carry):
        row = jnp.int32(0)
        for i in range(1, ROWS):
            row = jnp.where(owners[i] == d, i, row)
        sb[d] = hidv[row, pl.ds(mine, 16), :]
        return carry

    lax.fori_loop(0, NREP, fill, 0)

    pl.semaphore_wait(bar, NREP - 1 + TP - 1)

    def exchange(src, dst, n):
        def one(d):
            pltpu.make_async_remote_copy(
                src(d), dst.at[me], send_sem.at[n], recv_sem.at[n], device_id=(d, tp), device_id_type=MESH
            ).start()

        peers(one)
        pltpu.make_async_copy(src(me), dst.at[me], recv_sem.at[n]).start()

    def received(dst, n):
        pltpu.make_async_copy(dst, dst, recv_sem.at[n]).wait()

    exchange(lambda d: sb.at[d], arr, 0)
    exchange(lambda d: mb, mrec, 1)

    hf[...] = hidv[...].reshape(ROWS * LANES, LANES).astype(F32)
    for c in range(CHUNKS):
        both = [hf[pl.ds(2 * c + t, ROWS, stride=LANES), :] for t in range(2)]
        xl[:, c * LANES : (c + 1) * LANES] = jnp.concatenate(both, axis=0).astype(BF16)
    l_wk.wait()
    new_keys = jnp.dot(xl[...], wkv[...], preferred_element_type=F32)
    l_len.wait()
    row16 = lax.broadcasted_iota(I32, (2 * ROWS, LANES), 0)
    lane16 = lax.broadcasted_iota(I32, (2 * ROWS, LANES), 1)
    position = jnp.zeros((2 * ROWS, LANES), I32)
    for i in range(ROWS):
        for t in range(2):
            position = jnp.where(row16 == t * ROWS + i, length_s[0, i] + t, position)
    half = (lane16 % (LANES // 2)).astype(F32)
    angle = position.astype(F32) * jnp.exp(half * (-2.0 * LOG_BASE / LANES))
    turned = pltpu.roll(new_keys, LANES // 2, 1)
    sine = jnp.where(lane16 < LANES // 2, -jnp.sin(angle), jnp.sin(angle))
    nkf[...] = (new_keys * jnp.cos(angle) + turned * sine).astype(BF16).astype(F32)
    l_wv.wait()
    pvs[...] = jnp.dot(xl[...], wvv[...], preferred_element_type=F32)

    l_tab.wait()
    l_q.wait()
    l_k.wait()
    l_v.wait()
    scale = LANES ** (-0.5)
    span = ROWS * LANES
    token = lax.broadcasted_iota(I32, (16, 1), 0) % 2
    place = lax.broadcasted_iota(I32, (16, span), 1)

    def attend(r, carry):
        q = qv[r]
        pages = [table_s[r, n] for n in range(8)]
        keys = jnp.concatenate([kv[p] for p in pages], axis=0)
        old = lax.dot_general(q, keys, NT, preferred_element_type=F32) * scale
        old = jnp.where(place < length_s[0, r], old, -jnp.inf)
        qf = q.astype(F32)
        new0 = jnp.sum(qf * nkf[pl.ds(r, 1), :], axis=-1, keepdims=True) * scale
        new1 = jnp.sum(qf * nkf[pl.ds(ROWS + r, 1), :], axis=-1, keepdims=True) * scale
        new1 = jnp.where(token == 1, new1, -jnp.inf)
        peak = jnp.maximum(jnp.max(old, axis=-1, keepdims=True), jnp.maximum(new0, new1))
        eo, e0, e1 = jnp.exp(old - peak), jnp.exp(new0 - peak), jnp.exp(new1 - peak)
        total = jnp.sum(eo, axis=-1, keepdims=True) + e0 + e1
        weights = (eo / total).astype(BF16)
        values = jnp.concatenate([vv[p] for p in pages], axis=0)
        mixed[r] = jnp.dot(weights, values, preferred_element_type=F32)
        wn0s[r] = jnp.broadcast_to((e0 / total).astype(BF16).astype(F32), (16, LANES))
        wn1s[r] = jnp.broadcast_to((e1 / total).astype(BF16).astype(F32), (16, LANES))
        return carry

    lax.fori_loop(0, ROWS, attend, 0)

    targets = [s // SLOTS for s in slots]

    def order(d, carry):
        count, first, second = jnp.int32(0), jnp.int32(0), jnp.int32(0)
        for i in range(ROWS):
            here = targets[i] == d
            first = jnp.where(here & (count == 0), i, first)
            second = jnp.where(here & (count == 1), i, second)
            count = count + here.astype(I32)
        idx_s[d, 0] = first
        idx_s[d, 1] = second
        return carry

    lax.fori_loop(0, NREP, order, 0)

    received(mrec, 1)
    known = mrec[:, 0, :]
    lane32 = lax.broadcasted_iota(I32, (NREP, LANES), 1)
    own = ((known // ADP) == me) & (lane32 < ROWS)
    within = jnp.sum(jnp.where(own, (known % ADP).astype(F32), 0.0), axis=-1, keepdims=True).astype(I32)
    pick = jnp.concatenate([within, within], axis=0)
    block = lax.broadcasted_iota(I32, (2 * NREP, ADP * RANK), 1) // RANK
    chosen = block == pick
    received(arr, 0)
    l_dn.wait()
    af[...] = arr[...].reshape(NREP * 16, LANES).astype(F32)
    for c in range(8):
        for t in range(2):
            piece = af[pl.ds(2 * c + t, NREP, stride=16), :]
            xs[t * NREP : (t + 1) * NREP, c * LANES : (c + 1) * LANES] = piece.astype(BF16)
    every = lax.dot_general(xs[...], dnv[...].reshape(ADP * RANK, 8 * LANES), NT, preferred_element_type=F32)
    every = jnp.where(chosen, every, 0.0)
    folded = every[:, :LANES]
    for v in range(1, 8):
        folded = folded + every[:, v * LANES : (v + 1) * LANES]
    folded = folded + pltpu.roll(folded, RANK, 1)
    tb[...] = jnp.where(lane32 < RANK, folded[:NREP], folded[NREP:])

    def to_tp(d):
        pltpu.make_async_remote_copy(
            tb, trec.at[tp], send_sem.at[2], recv_sem.at[2], device_id=(me, d), device_id_type=MESH
        ).start()

    tp_peers(to_tp)
    pltpu.make_async_copy(tb, trec.at[tp], recv_sem.at[2]).start()

    target = known // SLOTS
    rank = jnp.zeros((NREP, LANES), I32)
    for back in range(1, ROWS):
        same = (pltpu.roll(target, back, 1) == target) & (lane32 >= ROWS + back)
        rank = rank + same.astype(I32)
    code = lax.broadcasted_iota(I32, (NREP, LANES), 0) * 2 + rank
    serving = (lane32 >= ROWS) & (lane32 < 2 * ROWS)
    for n in range(ROWS):
        hit = serving & (known == me * SLOTS + ROWS + n)
        code_s[n] = jnp.max(jnp.where(hit, code, -1))

    received(trec, 2)
    l_up.wait()
    low = trec[0]
    for n in range(1, TP):
        low = low + trec[n]
    low = low.astype(BF16).astype(F32)
    other = pltpu.roll(low, RANK, 1)
    spread = jnp.concatenate(
        [jnp.where(lane32 < RANK, low, other), jnp.where(lane32 < RANK, other, low)], axis=0
    )
    wide = jnp.where(chosen, jnp.concatenate([spread] * 8, axis=1), 0.0).astype(BF16)
    term = jnp.dot(wide, upv[...], preferred_element_type=F32)
    cs[:, 0, :] = term[:NREP]
    cs[:, 1, :] = term[NREP:]
    exchange(lambda d: cs.at[d], crec, 3)
    received(crec, 3)

    for r in range(ROWS):
        back = crec[owners[r]]
        value0 = (pvs[r : r + 1, :] + 0.5 * back[0:1]).astype(BF16).astype(F32)
        value1 = (pvs[ROWS + r : ROWS + r + 1, :] + 0.5 * back[1:2]).astype(BF16).astype(F32)
        served[r] = (mixed[r] + wn0s[r] * value0 + wn1s[r] * value1).astype(BF16)

    def moved(d, carry):
        sb4[d, 0] = served[idx_s[d, 0]]
        sb4[d, 1] = served[idx_s[d, 1]]
        return carry

    lax.fori_loop(0, NREP, moved, 0)
    exchange(lambda d: sb4.at[d], grec, 4)
    for r in range(ROWS):
        kept = slots[r] == me * SLOTS + r
        out[r] = jnp.where(kept, served[r], jnp.zeros((16, LANES), BF16))
    received(grec, 4)
    for n in range(ROWS):
        at = code_s[n]
        safe = jnp.clip(at, 0, 2 * NREP - 1)
        row = grec[safe // 2, safe % 2]
        out[ROWS + n] = jnp.where(at >= 0, row, jnp.zeros((16, LANES), BF16))

    def sent(ref, n):
        pltpu.make_async_copy(ref, ref, send_sem.at[n]).wait()

    sent(sb.at[pl.ds(0, NREP - 1)], 0)
    sent(mrec.at[pl.ds(0, NREP - 1)], 1)
    sent(trec.at[pl.ds(0, TP - 1)], 2)
    sent(cs.at[pl.ds(0, NREP - 1)], 3)
    sent(sb4.at[pl.ds(0, NREP - 1)], 4)


def shards(hidden, queries, wk, wv, down, up, ridx, home, table, lengths, serve, kc, vc):
    hid = hidden.reshape(ROWS, 2, CHUNKS, LANES).transpose(0, 2, 1, 3).reshape(ROWS, LANES, LANES)
    qin = queries.reshape(ROWS, 2, 8, LANES).transpose(0, 2, 1, 3).reshape(ROWS, 16, LANES)
    dn = jnp.swapaxes(down, 1, 2)
    upr = up.reshape(ADP * RANK, LANES)
    vmem, smem = pltpu.VMEM, pltpu.SMEM
    scratch = [
        vmem((ROWS, LANES, LANES), BF16), vmem((ROWS, 16, LANES), BF16), vmem((8192, LANES), BF16), vmem((8192, LANES), BF16),
        vmem((ADP, RANK, 1024), BF16), vmem((ADP * RANK, LANES), BF16), vmem((64, LANES, LANES), BF16), vmem((64, LANES, LANES), BF16),
        smem((8,), I32), smem((512,), I32), smem((8, 8), I32), smem((1, 8), I32), smem((8,), I32),
        vmem((ROWS * LANES, LANES), F32), vmem((16, 8192), BF16),
        vmem((NREP, 16, LANES), BF16), vmem((NREP, 16, LANES), BF16),
        vmem((NREP * 16, LANES), F32), vmem((2 * NREP, 1024), BF16),
        vmem((1, LANES), I32), vmem((NREP, 1, LANES), I32),
        vmem((NREP, LANES), F32), vmem((TP, NREP, LANES), F32),
        vmem((NREP, 2, LANES), F32), vmem((NREP, 2, LANES), F32),
        vmem((ROWS, 16, LANES), F32), vmem((ROWS, 16, LANES), F32), vmem((ROWS, 16, LANES), F32),
        vmem((16, LANES), F32), vmem((16, LANES), F32), vmem((ROWS, 16, LANES), BF16),
        vmem((NREP, 2, 16, LANES), BF16), vmem((NREP, 2, 16, LANES), BF16),
        smem((NREP, 2), I32), smem((ROWS,), I32),
        pltpu.SemaphoreType.DMA((13,)), pltpu.SemaphoreType.DMA((5,)), pltpu.SemaphoreType.DMA((5,)),
    ]
    result = pl.pallas_call(
        kernel,
        out_shape=jax.ShapeDtypeStruct((SLOTS, 16, LANES), BF16),
        in_specs=[pl.BlockSpec(memory_space=pltpu.HBM)] * 13,
        out_specs=pl.BlockSpec(memory_space=pltpu.VMEM),
        scratch_shapes=scratch,
        compiler_params=pltpu.CompilerParams(
            collective_id=0, has_side_effects=True, vmem_limit_bytes=67043328
        ),
        name="decode",
    )(hid, qin, wk, wv, dn, upr, ridx, home, table, lengths, serve, kc, vc)
    return result.reshape(SLOTS, 8, 2, LANES).transpose(0, 2, 1, 3).reshape(SLOTS, 2, 1024)


def solution(mesh):
    placed = (
        P("rep", None, None),
        P("rep", None, "tp"),
        P(None, "tp"),
        P(None, "tp"),
        P("rep", "tp", None),
        P("rep", None, "tp"),
        P("rep"),
        P(),
        P("rep", None),
        P("rep", None),
        P("rep"),
        P("rep", None, "tp"),
        P("rep", None, "tp"),
    )
    return jax.shard_map(
        shards, mesh=mesh, in_specs=placed, out_specs=P("rep", None, "tp"), check_vma=False
    )
```

time: 129 us -> 42.2 us (0.33)
  the two profiles are of different devices: /device:TPU:8 before, /device:TPU:1 now
where the time goes in v1:
time: 42.2 us; the launch traced here: 42.1 us
  Pallas kernels  40.6 us (96%)
  local copies, waits for them, and re-layouts  1.52 us (4%)
    pallas_call x1, Pallas kernels, shards(): pl.pallas_call(kernel, out_shape=jax.ShapeDtypeStruct((SLOTS, 16, LANES),...  40.6 us
    unnamed x1, local copies, waits for them, and re-layouts  1.52 us

profile of v1, /device:TPU:1, one launch (start us, length us, event | category | flops | bytes accessed | tf_op | source)
XLA Modules:
  0.0 42.1 jit_solution(13027726981160911432)
XLA Ops:
  0.0 40.6 %decode.1 = bf16[16,16,128]{2,1,0:T(8,128)(2,1)} custom-call(bf16[8,128,128]{2,1,0:T(8,128)(2,1)} %bitcast.19, bf16[8,16,128]{2,1,0:T(8,128)(2,1)} %bitcast.21, bf16[8192,128]{1,0:T(8,128)(2,1)} %wk.1, bf16[8192,128]{1,0:T(8,128)(2,1)} %wv.1, bf16[16,64,1024]{2,1,0:T(8,128)(2,1)} %bitcast.17, bf16[1024,128]{1,0:T(8,128)(2,1)} %bitcast.20, s32[8]{0:T(128)} %ridx.1, ...), custom_call_target="tpu_custom_call" | custom-call | tf_op jit(solution)/shard_map/decode/pallas_call | solution.py:287
  40.6 1.5 %copy.18 = bf16[16,2,1024]{2,1,0:T(2,128)(2,1)} copy(bf16[16,2,1024]{2,1,0:T(2,128)(2,1)} %bitcast.18) | data formatting | bytes 131072

commit v2 on v1

--- a/solution.py
+++ b/solution.py
@@ -24,8 +24,8 @@
     hid, qin, wk, wv, dn, up, ridx, home, table, length, serve, kc, vc,
     out,
     hidv, qv, wkv, wvv, dnv, upv, kv, vv, ridx_s, home_s, table_s, length_s, serve_s,
-    hf, xl, sb, arr, af, xs, mb, mrec, tb, trec, cs, crec, mixed, wn0s, wn1s, nkf, pvs, served, sb4, grec,
-    idx_s, code_s, in_sem, send_sem, recv_sem,
+    hf, xl, sb, arr, af, xs, mb, mrec, tb, trec, cs, crec, mixed, wn0s, wn1s, nkf, pvs, plain, pair_a, pair_b, sb4, grec,
+    route, sb3, mvrec, base, gain0, gain1, tab, tab_s, code_s, in_sem, send_sem, recv_sem,
 ):
     me = lax.axis_index("rep")
     tp = lax.axis_index("tp")
@@ -77,11 +77,25 @@
     l_hid.wait()
     mine = pl.multiple_of(tp * 16, 16)
 
+    targets = [s // SLOTS for s in slots]
+    none = jnp.zeros((1, LANES), I32)
+    to_home, first, second, count = none, none, none, none
+    for i in range(ROWS):
+        to_home = jnp.where(lane1 == owners[i], i, to_home)
+        here = lane1 == targets[i]
+        first = jnp.where(here & (count == 0), i, first)
+        second = jnp.where(here & (count == 1), i, second)
+        count = count + here.astype(I32)
+    tab[...] = jnp.zeros((8, LANES), I32)
+    tab[0:1, :] = to_home
+    tab[1:2, :] = first
+    tab[2:3, :] = second
+    to_smem = pltpu.make_async_copy(tab, tab_s, in_sem.at[13])
+    to_smem.start()
+    to_smem.wait()
+
     def fill(d, carry):
-        row = jnp.int32(0)
-        for i in range(1, ROWS):
-            row = jnp.where(owners[i] == d, i, row)
-        sb[d] = hidv[row, pl.ds(mine, 16), :]
+        sb[d] = hidv[tab_s[0, d], pl.ds(mine, 16), :]
         return carry
 
     lax.fori_loop(0, NREP, fill, 0)
@@ -149,26 +163,27 @@
         weights = (eo / total).astype(BF16)
         values = jnp.concatenate([vv[p] for p in pages], axis=0)
         mixed[r] = jnp.dot(weights, values, preferred_element_type=F32)
-        wn0s[r] = jnp.broadcast_to((e0 / total).astype(BF16).astype(F32), (16, LANES))
-        wn1s[r] = jnp.broadcast_to((e1 / total).astype(BF16).astype(F32), (16, LANES))
+        w0 = jnp.broadcast_to((e0 / total).astype(BF16).astype(F32), (16, LANES))
+        w1 = jnp.broadcast_to((e1 / total).astype(BF16).astype(F32), (16, LANES))
+        wn0s[r] = w0
+        wn1s[r] = w1
+        fresh = w0 * pvs[pl.ds(r, 1), :] + w1 * pvs[pl.ds(ROWS + r, 1), :]
+        plain[r] = (mixed[r] + fresh).astype(BF16)
+        pair_a[r] = jnp.where(lane16 == 0, w0, jnp.where(lane16 == 1, w1, 0.0)).astype(BF16)
+        pair_b[r] = jnp.where(lane16 == 2, w0, jnp.where(lane16 == 3, w1, 0.0)).astype(BF16)
         return carry
 
     lax.fori_loop(0, ROWS, attend, 0)
 
-    targets = [s // SLOTS for s in slots]
-
-    def order(d, carry):
-        count, first, second = jnp.int32(0), jnp.int32(0), jnp.int32(0)
-        for i in range(ROWS):
-            here = targets[i] == d
-            first = jnp.where(here & (count == 0), i, first)
-            second = jnp.where(here & (count == 1), i, second)
-            count = count + here.astype(I32)
-        idx_s[d, 0] = first
-        idx_s[d, 1] = second
+    def moved(d, carry):
+        one, two = tab_s[1, d], tab_s[2, d]
+        sb4[d, 0] = plain[one]
+        sb4[d, 1] = plain[two]
+        sb4[d, 2] = pair_a[one] + pair_b[two]
         return carry
 
-    lax.fori_loop(0, NREP, order, 0)
+    lax.fori_loop(0, NREP, moved, 0)
+    exchange(lambda d: sb4.at[d], grec, 4)
 
     received(mrec, 1)
     known = mrec[:, 0, :]
@@ -212,6 +227,15 @@
         hit = serving & (known == me * SLOTS + ROWS + n)
         code_s[n] = jnp.max(jnp.where(hit, code, -1))
 
+    goal = jnp.sum(jnp.where(pltpu.roll(own.astype(I32), ROWS, 1) > 0, known, 0).astype(F32), axis=-1, keepdims=True)
+    held = jnp.sum(own.astype(F32), axis=-1, keepdims=True)
+    goal = jnp.where(held > 0.0, goal, -1.0)
+    goal = jnp.broadcast_to(jnp.concatenate([goal, goal], axis=0), (2 * NREP, LANES)).T[0:1, :]
+    line = lax.broadcasted_iota(I32, (NREP * 16, 2 * NREP), 0)
+    from_token = lax.broadcasted_iota(I32, (NREP * 16, 2 * NREP), 1) // NREP
+    wanted = (line // 16) * SLOTS + ROWS + (line % 16) // 2
+    route[...] = jnp.where((goal == wanted.astype(F32)) & (from_token == line % 2), 1.0, 0.0).astype(BF16)
+
     received(trec, 2)
     l_up.wait()
     low = trec[0]
@@ -226,31 +250,36 @@
     term = jnp.dot(wide, upv[...], preferred_element_type=F32)
     cs[:, 0, :] = term[:NREP]
     cs[:, 1, :] = term[NREP:]
+    spread_out = jnp.dot(route[...], term.astype(BF16), preferred_element_type=F32)
+    sb3[...] = spread_out.astype(BF16).reshape(NREP, 16, LANES)
+    exchange(lambda d: sb3.at[d], mvrec, 5)
     exchange(lambda d: cs.at[d], crec, 3)
+
+    received(grec, 4)
+    for n in range(ROWS):
+        at = code_s[n]
+        safe = jnp.clip(at, 0, 2 * NREP - 1)
+        pair = grec[safe // 2, 2].astype(F32)
+        odd = safe % 2 == 1
+        there = at >= 0
+        base[n] = jnp.where(there, grec[safe // 2, safe % 2].astype(F32), 0.0)
+        gain0[n] = jnp.broadcast_to(jnp.where(odd, pair[:, 2:3], pair[:, 0:1]) * 0.5, (16, LANES))
+        gain1[n] = jnp.broadcast_to(jnp.where(odd, pair[:, 3:4], pair[:, 1:2]) * 0.5, (16, LANES))
     received(crec, 3)
-
     for r in range(ROWS):
         back = crec[owners[r]]
         value0 = (pvs[r : r + 1, :] + 0.5 * back[0:1]).astype(BF16).astype(F32)
         value1 = (pvs[ROWS + r : ROWS + r + 1, :] + 0.5 * back[1:2]).astype(BF16).astype(F32)
-        served[r] = (mixed[r] + wn0s[r] * value0 + wn1s[r] * value1).astype(BF16)
-
-    def moved(d, carry):
-        sb4[d, 0] = served[idx_s[d, 0]]
-        sb4[d, 1] = served[idx_s[d, 1]]
-        return carry
-
-    lax.fori_loop(0, NREP, moved, 0)
-    exchange(lambda d: sb4.at[d], grec, 4)
-    for r in range(ROWS):
+        done = (mixed[r] + wn0s[r] * value0 + wn1s[r] * value1).astype(BF16)
         kept = slots[r] == me * SLOTS + r
-        out[r] = jnp.where(kept, served[r], jnp.zeros((16, LANES), BF16))
-    received(grec, 4)
+        out[r] = jnp.where(kept, done, jnp.zeros((16, LANES), BF16))
+    received(mvrec, 5)
+    extra = mvrec[0].astype(F32)
+    for n in range(1, NREP):
+        extra = extra + mvrec[n].astype(F32)
     for n in range(ROWS):
-        at = code_s[n]
-        safe = jnp.clip(at, 0, 2 * NREP - 1)
-        row = grec[safe // 2, safe % 2]
-        out[ROWS + n] = jnp.where(at >= 0, row, jnp.zeros((16, LANES), BF16))
+        added = gain0[n] * extra[2 * n : 2 * n + 1] + gain1[n] * extra[2 * n + 1 : 2 * n + 2]
+        out[ROWS + n] = (base[n] + added).astype(BF16)
 
     def sent(ref, n):
         pltpu.make_async_copy(ref, ref, send_sem.at[n]).wait()
@@ -260,6 +289,7 @@
     sent(trec.at[pl.ds(0, TP - 1)], 2)
     sent(cs.at[pl.ds(0, NREP - 1)], 3)
     sent(sb4.at[pl.ds(0, NREP - 1)], 4)
+    sent(sb3.at[pl.ds(0, NREP - 1)], 5)
 
 
 def shards(hidden, queries, wk, wv, down, up, ridx, home, table, lengths, serve, kc, vc):
@@ -279,10 +309,13 @@
         vmem((NREP, LANES), F32), vmem((TP, NREP, LANES), F32),
         vmem((NREP, 2, LANES), F32), vmem((NREP, 2, LANES), F32),
         vmem((ROWS, 16, LANES), F32), vmem((ROWS, 16, LANES), F32), vmem((ROWS, 16, LANES), F32),
-        vmem((16, LANES), F32), vmem((16, LANES), F32), vmem((ROWS, 16, LANES), BF16),
-        vmem((NREP, 2, 16, LANES), BF16), vmem((NREP, 2, 16, LANES), BF16),
-        smem((NREP, 2), I32), smem((ROWS,), I32),
-        pltpu.SemaphoreType.DMA((13,)), pltpu.SemaphoreType.DMA((5,)), pltpu.SemaphoreType.DMA((5,)),
+        vmem((16, LANES), F32), vmem((16, LANES), F32),
+        vmem((ROWS, 16, LANES), BF16), vmem((ROWS, 16, LANES), BF16), vmem((ROWS, 16, LANES), BF16),
+        vmem((NREP, 3, 16, LANES), BF16), vmem((NREP, 3, 16, LANES), BF16),
+        vmem((NREP * 16, 2 * NREP), BF16), vmem((NREP, 16, LANES), BF16), vmem((NREP, 16, LANES), BF16),
+        vmem((ROWS, 16, LANES), F32), vmem((ROWS, 16, LANES), F32), vmem((ROWS, 16, LANES), F32),
+        vmem((8, LANES), I32), smem((8, LANES), I32), smem((ROWS,), I32),
+        pltpu.SemaphoreType.DMA((14,)), pltpu.SemaphoreType.DMA((6,)), pltpu.SemaphoreType.DMA((6,)),
     ]
     result = pl.pallas_call(
         kernel,

time: 42.2 us -> 35.8 us (0.85)
  Pallas kernels: 40.6 us -> 34.2 us
    pallas_call x1, Pallas kernels: 40.6 us -> 34.2 us  [shards(): pl.pallas_call(kernel, out_shape=jax.ShapeDtypeStruct((SLOTS, 16, LANES),...]
where the time goes in v2:
time: 35.8 us; the launch traced here: 35.7 us
  Pallas kernels  34.2 us (96%)
  local copies, waits for them, and re-layouts  1.52 us (4%)
    pallas_call x1, Pallas kernels, shards(): pl.pallas_call(kernel, out_shape=jax.ShapeDtypeStruct((SLOTS, 16, LANES),...  34.2 us
    unnamed x1, local copies, waits for them, and re-layouts  1.52 us

profile of v2, /device:TPU:1, one launch (start us, length us, event | category | flops | bytes accessed | tf_op | source)
XLA Modules:
  0.0 35.7 jit_solution(3463727093902988000)
XLA Ops:
  0.0 34.2 %decode.1 = bf16[16,16,128]{2,1,0:T(8,128)(2,1)} custom-call(bf16[8,128,128]{2,1,0:T(8,128)(2,1)} %bitcast.19, bf16[8,16,128]{2,1,0:T(8,128)(2,1)} %bitcast.21, bf16[8192,128]{1,0:T(8,128)(2,1)} %wk.1, bf16[8192,128]{1,0:T(8,128)(2,1)} %wv.1, bf16[16,64,1024]{2,1,0:T(8,128)(2,1)} %bitcast.17, bf16[1024,128]{1,0:T(8,128)(2,1)} %bitcast.20, s32[8]{0:T(128)} %ridx.1, ...), custom_call_target="tpu_custom_call" | custom-call | tf_op jit(solution)/shard_map/decode/pallas_call | solution.py:320
  34.2 1.5 %copy.18 = bf16[16,2,1024]{2,1,0:T(2,128)(2,1)} copy(bf16[16,2,1024]{2,1,0:T(2,128)(2,1)} %bitcast.18) | data formatting | bytes 131072

commit v3 on v2

--- a/solution.py
+++ b/solution.py
@@ -18,36 +18,33 @@
 CHUNKS = 64
 NT = (((1,), (1,)), ((), ()))
 LOG_BASE = math.log(1000000.0)
+FAR_FIRST = sorted(
+    [(x, z) for x in range(NX) for z in range(NZ) if x or z],
+    key=lambda o: -(min(o[0], NX - o[0]) + min(o[1], NZ - o[1])),
+)
 
 
 def kernel(
     hid, qin, wk, wv, dn, up, ridx, home, table, length, serve, kc, vc,
     out,
     hidv, qv, wkv, wvv, dnv, upv, kv, vv, ridx_s, home_s, table_s, length_s, serve_s,
-    hf, xl, sb, arr, af, xs, mb, mrec, tb, trec, cs, crec, mixed, wn0s, wn1s, nkf, pvs, plain, pair_a, pair_b, sb4, grec,
-    route, sb3, mvrec, base, gain0, gain1, tab, tab_s, code_s, in_sem, send_sem, recv_sem,
+    hf, xl, sb, arr, af, xs, mb, mrec, tb, trec, cs, crec, mixed, wn0s, wn1s, nkf, pvs, plain, gains, wb, wrec, sb4, grec,
+    route, sb3, mvrec, base, gain0, gain1, tab, tab_s, code_s, line_s, wq, in_sem, send_sem, recv_sem,
 ):
     me = lax.axis_index("rep")
     tp = lax.axis_index("tp")
     mx, mz = me // NZ, me % NZ
 
-    def far(a):
-        return ((mx + 2 + a % NX) % NX) * NZ + (mz + 4 + a // NX) % NZ
+    to_x = [((mx + n) % NX) * NZ for n in range(NX)]
+    to_z = [(mz + n) % NZ for n in range(NZ)]
 
     def peers(do):
-        def step(a, carry):
-            do(far(a))
-            return carry
-
-        lax.fori_loop(0, 18, step, 0)
-        lax.fori_loop(19, 32, step, 0)
+        for dx, dz in FAR_FIRST:
+            do(to_x[dx] + to_z[dz])
 
     def tp_peers(do):
-        def step(a, carry):
+        for a in (4, 5, 3, 2, 6, 1, 7):
             do((tp + a) % TP)
-            return carry
-
-        lax.fori_loop(1, TP, step, 0)
 
     bar = pltpu.get_barrier_semaphore()
     peers(lambda d: pl.semaphore_signal(bar, inc=1, device_id=(d, tp), device_id_type=MESH))
@@ -55,13 +52,18 @@
 
     pairs = [
         (ridx, ridx_s), (home, home_s), (serve, serve_s), (hid, hidv), (length, length_s), (table, table_s),
-        (wk, wkv), (qin, qv), (kc, kv), (vc, vv), (wv, wvv), (dn, dnv), (up, upv),
+        (wk, wkv), (wv, wvv), (qin, qv), (kc, kv), (vc, vv), (dn, dnv), (up, upv),
     ]
     loads = [pltpu.make_async_copy(s, d, in_sem.at[n]) for n, (s, d) in enumerate(pairs)]
     for c in loads:
         c.start()
-    (l_ridx, l_home, l_serve, l_hid, l_len, l_tab, l_wk, l_q, l_k, l_v, l_wv, l_dn, l_up) = loads
-
+    (l_ridx, l_home, l_serve, l_hid, l_len, l_tab, l_wk, l_wv, l_q, l_k, l_v, l_dn, l_up) = loads
+
+    l_hid.wait()
+    hf[...] = hidv[...].reshape(ROWS * LANES, LANES).astype(F32)
+    for c in range(CHUNKS):
+        both = [hf[pl.ds(2 * c + t, ROWS, stride=LANES), :] for t in range(2)]
+        xl[:, c * LANES : (c + 1) * LANES] = jnp.concatenate(both, axis=0).astype(BF16)
     l_ridx.wait()
     l_home.wait()
     l_serve.wait()
@@ -74,7 +76,6 @@
         meta = jnp.where(lane1 == i, homes[i], meta)
         meta = jnp.where(lane1 == ROWS + i, slots[i], meta)
     mb[...] = meta
-    l_hid.wait()
     mine = pl.multiple_of(tp * 16, 16)
 
     targets = [s // SLOTS for s in slots]
@@ -92,35 +93,6 @@
     tab[2:3, :] = second
     to_smem = pltpu.make_async_copy(tab, tab_s, in_sem.at[13])
     to_smem.start()
-    to_smem.wait()
-
-    def fill(d, carry):
-        sb[d] = hidv[tab_s[0, d], pl.ds(mine, 16), :]
-        return carry
-
-    lax.fori_loop(0, NREP, fill, 0)
-
-    pl.semaphore_wait(bar, NREP - 1 + TP - 1)
-
-    def exchange(src, dst, n):
-        def one(d):
-            pltpu.make_async_remote_copy(
-                src(d), dst.at[me], send_sem.at[n], recv_sem.at[n], device_id=(d, tp), device_id_type=MESH
-            ).start()
-
-        peers(one)
-        pltpu.make_async_copy(src(me), dst.at[me], recv_sem.at[n]).start()
-
-    def received(dst, n):
-        pltpu.make_async_copy(dst, dst, recv_sem.at[n]).wait()
-
-    exchange(lambda d: sb.at[d], arr, 0)
-    exchange(lambda d: mb, mrec, 1)
-
-    hf[...] = hidv[...].reshape(ROWS * LANES, LANES).astype(F32)
-    for c in range(CHUNKS):
-        both = [hf[pl.ds(2 * c + t, ROWS, stride=LANES), :] for t in range(2)]
-        xl[:, c * LANES : (c + 1) * LANES] = jnp.concatenate(both, axis=0).astype(BF16)
     l_wk.wait()
     new_keys = jnp.dot(xl[...], wkv[...], preferred_element_type=F32)
     l_len.wait()
@@ -137,6 +109,32 @@
     nkf[...] = (new_keys * jnp.cos(angle) + turned * sine).astype(BF16).astype(F32)
     l_wv.wait()
     pvs[...] = jnp.dot(xl[...], wvv[...], preferred_element_type=F32)
+
+    to_smem.wait()
+
+    def fill(d, carry):
+        sb[d] = hidv[tab_s[0, d], pl.ds(mine, 16), :]
+        return carry
+
+    lax.fori_loop(0, NREP, fill, 0)
+
+    pl.semaphore_wait(bar, NREP - 1 + TP - 1)
+
+    def exchange(*moves):
+        def one(d):
+            for src, dst, n in moves:
+                pltpu.make_async_remote_copy(
+                    src(d), dst.at[me], send_sem.at[n], recv_sem.at[n], device_id=(d, tp), device_id_type=MESH
+                ).start()
+
+        peers(one)
+        for src, dst, n in moves:
+            pltpu.make_async_copy(src(me), dst.at[me], recv_sem.at[n]).start()
+
+    def received(dst, n):
+        pltpu.make_async_copy(dst, dst, recv_sem.at[n]).wait()
+
+    exchange((lambda d: sb.at[d], arr, 0), (lambda d: mb, mrec, 1))
 
     l_tab.wait()
     l_q.wait()
@@ -169,21 +167,25 @@
         wn1s[r] = w1
         fresh = w0 * pvs[pl.ds(r, 1), :] + w1 * pvs[pl.ds(ROWS + r, 1), :]
         plain[r] = (mixed[r] + fresh).astype(BF16)
-        pair_a[r] = jnp.where(lane16 == 0, w0, jnp.where(lane16 == 1, w1, 0.0)).astype(BF16)
-        pair_b[r] = jnp.where(lane16 == 2, w0, jnp.where(lane16 == 3, w1, 0.0)).astype(BF16)
+        gains[r] = jnp.where(lane16 == 0, w0, w1)
         return carry
 
-    lax.fori_loop(0, ROWS, attend, 0)
+    def several(n, carry):
+        for u in range(4):
+            attend(n * 4 + u, carry)
+        return carry
+
+    lax.fori_loop(0, ROWS // 4, several, 0)
 
     def moved(d, carry):
         one, two = tab_s[1, d], tab_s[2, d]
         sb4[d, 0] = plain[one]
         sb4[d, 1] = plain[two]
-        sb4[d, 2] = pair_a[one] + pair_b[two]
         return carry
 
+    wb[...] = gains[...].reshape(ROWS * 16, LANES).T[0:2, :]
     lax.fori_loop(0, NREP, moved, 0)
-    exchange(lambda d: sb4.at[d], grec, 4)
+    exchange((lambda d: sb4.at[d], grec, 4), (lambda d: wb, wrec, 2))
 
     received(mrec, 1)
     known = mrec[:, 0, :]
@@ -210,11 +212,11 @@
 
     def to_tp(d):
         pltpu.make_async_remote_copy(
-            tb, trec.at[tp], send_sem.at[2], recv_sem.at[2], device_id=(me, d), device_id_type=MESH
+            tb, trec.at[tp], send_sem.at[6], recv_sem.at[6], device_id=(me, d), device_id_type=MESH
         ).start()
 
     tp_peers(to_tp)
-    pltpu.make_async_copy(tb, trec.at[tp], recv_sem.at[2]).start()
+    pltpu.make_async_copy(tb, trec.at[tp], recv_sem.at[6]).start()
 
     target = known // SLOTS
     rank = jnp.zeros((NREP, LANES), I32)
@@ -226,6 +228,7 @@
     for n in range(ROWS):
         hit = serving & (known == me * SLOTS + ROWS + n)
         code_s[n] = jnp.max(jnp.where(hit, code, -1))
+        line_s[n] = jnp.max(jnp.where(hit, lane32 - ROWS, 0))
 
     goal = jnp.sum(jnp.where(pltpu.roll(own.astype(I32), ROWS, 1) > 0, known, 0).astype(F32), axis=-1, keepdims=True)
     held = jnp.sum(own.astype(F32), axis=-1, keepdims=True)
@@ -236,7 +239,7 @@
     wanted = (line // 16) * SLOTS + ROWS + (line % 16) // 2
     route[...] = jnp.where((goal == wanted.astype(F32)) & (from_token == line % 2), 1.0, 0.0).astype(BF16)
 
-    received(trec, 2)
+    received(trec, 6)
     l_up.wait()
     low = trec[0]
     for n in range(1, TP):
@@ -252,19 +255,20 @@
     cs[:, 1, :] = term[NREP:]
     spread_out = jnp.dot(route[...], term.astype(BF16), preferred_element_type=F32)
     sb3[...] = spread_out.astype(BF16).reshape(NREP, 16, LANES)
-    exchange(lambda d: sb3.at[d], mvrec, 5)
-    exchange(lambda d: cs.at[d], crec, 3)
+    exchange((lambda d: sb3.at[d], mvrec, 5), (lambda d: cs.at[d], crec, 3))
 
     received(grec, 4)
+    received(wrec, 2)
     for n in range(ROWS):
-        at = code_s[n]
-        safe = jnp.clip(at, 0, 2 * NREP - 1)
-        pair = grec[safe // 2, 2].astype(F32)
-        odd = safe % 2 == 1
-        there = at >= 0
-        base[n] = jnp.where(there, grec[safe // 2, safe % 2].astype(F32), 0.0)
-        gain0[n] = jnp.broadcast_to(jnp.where(odd, pair[:, 2:3], pair[:, 0:1]) * 0.5, (16, LANES))
-        gain1[n] = jnp.broadcast_to(jnp.where(odd, pair[:, 3:4], pair[:, 1:2]) * 0.5, (16, LANES))
+        safe = jnp.clip(code_s[n], 0, 2 * NREP - 1)
+        shift = (LANES - jnp.clip(line_s[n], 0, ROWS - 1) * 16) % LANES
+        wq[2 * n : 2 * n + 2, :] = pltpu.roll(wrec[safe // 2], shift, 1)
+    column = wq[...].T[0:16, :] * 0.5
+    for n in range(ROWS):
+        safe = jnp.clip(code_s[n], 0, 2 * NREP - 1)
+        base[n] = jnp.where(code_s[n] >= 0, grec[safe // 2, safe % 2].astype(F32), 0.0)
+        gain0[n] = jnp.broadcast_to(column[:, 2 * n : 2 * n + 1], (16, LANES))
+        gain1[n] = jnp.broadcast_to(column[:, 2 * n + 1 : 2 * n + 2], (16, LANES))
     received(crec, 3)
     for r in range(ROWS):
         back = crec[owners[r]]
@@ -286,7 +290,8 @@
 
     sent(sb.at[pl.ds(0, NREP - 1)], 0)
     sent(mrec.at[pl.ds(0, NREP - 1)], 1)
-    sent(trec.at[pl.ds(0, TP - 1)], 2)
+    sent(trec.at[pl.ds(0, TP - 1)], 6)
+    sent(wrec.at[pl.ds(0, NREP - 1)], 2)
     sent(cs.at[pl.ds(0, NREP - 1)], 3)
     sent(sb4.at[pl.ds(0, NREP - 1)], 4)
     sent(sb3.at[pl.ds(0, NREP - 1)], 5)
@@ -310,12 +315,12 @@
         vmem((NREP, 2, LANES), F32), vmem((NREP, 2, LANES), F32),
         vmem((ROWS, 16, LANES), F32), vmem((ROWS, 16, LANES), F32), vmem((ROWS, 16, LANES), F32),
         vmem((16, LANES), F32), vmem((16, LANES), F32),
-        vmem((ROWS, 16, LANES), BF16), vmem((ROWS, 16, LANES), BF16), vmem((ROWS, 16, LANES), BF16),
-        vmem((NREP, 3, 16, LANES), BF16), vmem((NREP, 3, 16, LANES), BF16),
+        vmem((ROWS, 16, LANES), BF16), vmem((ROWS, 16, LANES), F32), vmem((2, LANES), F32), vmem((NREP, 2, LANES), F32),
+        vmem((NREP, 2, 16, LANES), BF16), vmem((NREP, 2, 16, LANES), BF16),
         vmem((NREP * 16, 2 * NREP), BF16), vmem((NREP, 16, LANES), BF16), vmem((NREP, 16, LANES), BF16),
         vmem((ROWS, 16, LANES), F32), vmem((ROWS, 16, LANES), F32), vmem((ROWS, 16, LANES), F32),
-        vmem((8, LANES), I32), smem((8, LANES), I32), smem((ROWS,), I32),
-        pltpu.SemaphoreType.DMA((14,)), pltpu.SemaphoreType.DMA((6,)), pltpu.SemaphoreType.DMA((6,)),
+        vmem((8, LANES), I32), smem((8, LANES), I32), smem((ROWS,), I32), smem((ROWS,), I32), vmem((16, LANES), F32),
+        pltpu.SemaphoreType.DMA((14,)), pltpu.SemaphoreType.DMA((7,)), pltpu.SemaphoreType.DMA((7,)),
     ]
     result = pl.pallas_call(
         kernel,

time: 35.8 us -> 33.2 us (0.927)
  Pallas kernels: 34.2 us -> 31.5 us
    pallas_call x1, Pallas kernels: 34.2 us -> 31.5 us  [shards(): pl.pallas_call(kernel, out_shape=jax.ShapeDtypeStruct((SLOTS, 16, LANES),...]
where the time goes in v3:
time: 33.2 us; the launch traced here: 33.1 us
  Pallas kernels  31.5 us (95%)
  local copies, waits for them, and re-layouts  1.52 us (5%)
    pallas_call x1, Pallas kernels, shards(): pl.pallas_call(kernel, out_shape=jax.ShapeDtypeStruct((SLOTS, 16, LANES),...  31.5 us
    unnamed x1, local copies, waits for them, and re-layouts  1.52 us

profile of v3, /device:TPU:1, one launch (start us, length us, event | category | flops | bytes accessed | tf_op | source)
XLA Modules:
  0.0 33.1 jit_solution(3260154736539392600)
XLA Ops:
  0.0 31.5 %decode.1 = bf16[16,16,128]{2,1,0:T(8,128)(2,1)} custom-call(bf16[8,128,128]{2,1,0:T(8,128)(2,1)} %bitcast.19, bf16[8,16,128]{2,1,0:T(8,128)(2,1)} %bitcast.21, bf16[8192,128]{1,0:T(8,128)(2,1)} %wk.1, bf16[8192,128]{1,0:T(8,128)(2,1)} %wv.1, bf16[16,64,1024]{2,1,0:T(8,128)(2,1)} %bitcast.17, bf16[1024,128]{1,0:T(8,128)(2,1)} %bitcast.20, s32[8]{0:T(128)} %ridx.1, ...), custom_call_target="tpu_custom_call" | custom-call | tf_op jit(solution)/shard_map/decode/pallas_call | solution.py:325
  31.5 1.5 %copy.18 = bf16[16,2,1024]{2,1,0:T(2,128)(2,1)} copy(bf16[16,2,1024]{2,1,0:T(2,128)(2,1)} %bitcast.18) | data formatting | bytes 131072

commit v4 on v3

--- a/solution.py
+++ b/solution.py
@@ -255,7 +255,8 @@
     cs[:, 1, :] = term[NREP:]
     spread_out = jnp.dot(route[...], term.astype(BF16), preferred_element_type=F32)
     sb3[...] = spread_out.astype(BF16).reshape(NREP, 16, LANES)
-    exchange((lambda d: sb3.at[d], mvrec, 5), (lambda d: cs.at[d], crec, 3))
+    exchange((lambda d: cs.at[d], crec, 3))
+    exchange((lambda d: sb3.at[d], mvrec, 5))
 
     received(grec, 4)
     received(wrec, 2)
@@ -322,6 +323,7 @@
         vmem((8, LANES), I32), smem((8, LANES), I32), smem((ROWS,), I32), smem((ROWS,), I32), vmem((16, LANES), F32),
         pltpu.SemaphoreType.DMA((14,)), pltpu.SemaphoreType.DMA((7,)), pltpu.SemaphoreType.DMA((7,)),
     ]
+    hid, qin, wk, wv, dn, upr, ridx, home, table, lengths, serve, kc, vc = (pltpu.with_memory_space_constraint(a, pltpu.HBM) for a in (hid, qin, wk, wv, dn, upr, ridx, home, table, lengths, serve, kc, vc))
     result = pl.pallas_call(
         kernel,
         out_shape=jax.ShapeDtypeStruct((SLOTS, 16, LANES), BF16),
@@ -329,7 +331,7 @@
         out_specs=pl.BlockSpec(memory_space=pltpu.VMEM),
         scratch_shapes=scratch,
         compiler_params=pltpu.CompilerParams(
-            collective_id=0, has_side_effects=True, vmem_limit_bytes=67043328
+            collective_id=0, has_side_effects=True, vmem_limit_bytes=48 << 20
         ),
         name="decode",
     )(hid, qin, wk, wv, dn, upr, ridx, home, table, lengths, serve, kc, vc)

time: 33.2 us -> 31.4 us (0.946)
  local copies, waits for them, and re-layouts: 1.52 us -> 0.63 us
  Pallas kernels: 31.5 us -> 30.7 us
    unnamed x1, local copies, waits for them, and re-layouts: 1.52 us -> 0.63 us
    pallas_call x1, Pallas kernels: 31.5 us -> 30.7 us  [shards(): pl.pallas_call(kernel, out_shape=jax.ShapeDtypeStruct((SLOTS, 16, LANES),...]
where the time goes in v4:
time: 31.4 us
  Pallas kernels  30.7 us (98%)
  local copies, waits for them, and re-layouts  0.63 us (2%)
    pallas_call x1, Pallas kernels, shards(): pl.pallas_call(kernel, out_shape=jax.ShapeDtypeStruct((SLOTS, 16, LANES),...  30.7 us
    unnamed x1, local copies, waits for them, and re-layouts  0.63 us

profile of v4, /device:TPU:1, one launch (start us, length us, event | category | flops | bytes accessed | tf_op | source)
XLA Modules:
  0.0 31.4 jit_solution(5303544467804243123)
XLA Ops:
  0.0 30.7 %decode.1 = bf16[16,16,128]{2,1,0:T(8,128)(2,1)S(1)} custom-call(bf16[8,128,128]{2,1,0:T(8,128)(2,1)} %bitcast.19, bf16[8,16,128]{2,1,0:T(8,128)(2,1)} %bitcast.21, bf16[8192,128]{1,0:T(8,128)(2,1)} %wk.1, bf16[8192,128]{1,0:T(8,128)(2,1)} %wv.1, bf16[16,64,1024]{2,1,0:T(8,128)(2,1)} %bitcast.18, bf16[1024,128]{1,0:T(8,128)(2,1)} %bitcast.20, s32[8]{0:T(128)} %ridx.1, ...), custom_call_target="tpu_custom_call" | custom-call | tf_op jit(solution)/shard_map/decode/pallas_call | solution.py:327
  30.7 0.6 %copy.18 = bf16[16,2,1024]{2,1,0:T(2,128)(2,1)} copy(bf16[16,2,1024]{2,1,0:T(2,128)(2,1)S(1)} %bitcast.17) | data formatting | bytes 131072

commit v5 on v4

--- a/solution.py
+++ b/solution.py
@@ -28,7 +28,7 @@
     hid, qin, wk, wv, dn, up, ridx, home, table, length, serve, kc, vc,
     out,
     hidv, qv, wkv, wvv, dnv, upv, kv, vv, ridx_s, home_s, table_s, length_s, serve_s,
-    hf, xl, sb, arr, af, xs, mb, mrec, tb, trec, cs, crec, mixed, wn0s, wn1s, nkf, pvs, plain, gains, wb, wrec, sb4, grec,
+    hf, xl, sb, arr, af, ai, xs, mb, mrec, tb, trec, mixed, wn0s, wn1s, nkf, pvs, plain, gains, sb4, grec,
     route, sb3, mvrec, base, gain0, gain1, tab, tab_s, code_s, line_s, wq, in_sem, send_sem, recv_sem,
 ):
     me = lax.axis_index("rep")
@@ -73,9 +73,13 @@
     lane1 = lax.broadcasted_iota(I32, (1, LANES), 1)
     meta = jnp.zeros((1, LANES), I32)
     for i in range(ROWS):
-        meta = jnp.where(lane1 == i, homes[i], meta)
-        meta = jnp.where(lane1 == ROWS + i, slots[i], meta)
-    mb[...] = meta
+        for n, value in enumerate((owners[i], slots[i] // SLOTS, homes[i] % ADP, slots[i] % SLOTS)):
+            meta = jnp.where(lane1 == n * ROWS + i, value, meta)
+    line = jnp.full((1, LANES), -1, I32)
+    for i in range(ROWS):
+        line = jnp.where(lane1 == i, slots[i], line)
+    mb[...] = line
+    meta = jnp.broadcast_to(meta.astype(F32), (16, LANES)).astype(BF16)
     mine = pl.multiple_of(tp * 16, 16)
 
     targets = [s // SLOTS for s in slots]
@@ -113,28 +117,38 @@
     to_smem.wait()
 
     def fill(d, carry):
-        sb[d] = hidv[tab_s[0, d], pl.ds(mine, 16), :]
+        sb[d, 0:16] = hidv[tab_s[0, d], pl.ds(mine, 16), :]
+        sb[d, 16:32] = meta
         return carry
 
     lax.fori_loop(0, NREP, fill, 0)
 
     pl.semaphore_wait(bar, NREP - 1 + TP - 1)
 
-    def exchange(*moves):
+    def exchange(src, dst, lines, n):
+        part = pl.ds(0, lines)
+
         def one(d):
-            for src, dst, n in moves:
-                pltpu.make_async_remote_copy(
-                    src(d), dst.at[me], send_sem.at[n], recv_sem.at[n], device_id=(d, tp), device_id_type=MESH
-                ).start()
+            pltpu.make_async_remote_copy(
+                src.at[d, part], dst.at[me, part], send_sem.at[n], recv_sem.at[n], device_id=(d, tp), device_id_type=MESH
+            ).start()
 
         peers(one)
-        for src, dst, n in moves:
-            pltpu.make_async_copy(src(me), dst.at[me], recv_sem.at[n]).start()
-
-    def received(dst, n):
-        pltpu.make_async_copy(dst, dst, recv_sem.at[n]).wait()
-
-    exchange((lambda d: sb.at[d], arr, 0), (lambda d: mb, mrec, 1))
+        pltpu.make_async_copy(src.at[me, part], dst.at[me, part], recv_sem.at[n]).start()
+
+    def received(dst, lines, n):
+        every = dst.at[:, pl.ds(0, lines)]
+        pltpu.make_async_copy(every, every, recv_sem.at[n]).wait()
+
+    exchange(sb, arr, 18, 0)
+
+    def tell(d):
+        pltpu.make_async_remote_copy(
+            mb, mrec.at[me], send_sem.at[4], recv_sem.at[4], device_id=(d, tp), device_id_type=MESH
+        ).start()
+
+    peers(tell)
+    pltpu.make_async_copy(mb, mrec.at[me], recv_sem.at[4]).start()
 
     l_tab.wait()
     l_q.wait()
@@ -177,32 +191,36 @@
 
     lax.fori_loop(0, ROWS // 4, several, 0)
 
+    gain_lines = gains[...].reshape(ROWS * 16, LANES).T[0:16, :].astype(BF16)
+
     def moved(d, carry):
         one, two = tab_s[1, d], tab_s[2, d]
-        sb4[d, 0] = plain[one]
-        sb4[d, 1] = plain[two]
+        sb4[d, 0:16] = plain[one]
+        sb4[d, 16:32] = plain[two]
+        sb4[d, 32:48] = gain_lines
         return carry
 
-    wb[...] = gains[...].reshape(ROWS * 16, LANES).T[0:2, :]
     lax.fori_loop(0, NREP, moved, 0)
-    exchange((lambda d: sb4.at[d], grec, 4), (lambda d: wb, wrec, 2))
-
-    received(mrec, 1)
-    known = mrec[:, 0, :]
-    lane32 = lax.broadcasted_iota(I32, (NREP, LANES), 1)
-    own = ((known // ADP) == me) & (lane32 < ROWS)
-    within = jnp.sum(jnp.where(own, (known % ADP).astype(F32), 0.0), axis=-1, keepdims=True).astype(I32)
-    pick = jnp.concatenate([within, within], axis=0)
-    block = lax.broadcasted_iota(I32, (2 * NREP, ADP * RANK), 1) // RANK
-    chosen = block == pick
-    received(arr, 0)
+    exchange(sb4, grec, 34, 1)
+
     l_dn.wait()
-    af[...] = arr[...].reshape(NREP * 16, LANES).astype(F32)
+    l_up.wait()
+    received(arr, 18, 0)
+    af[...] = arr[:, 0:16, :].reshape(NREP * 16, LANES).astype(F32)
+    ai[...] = arr[:, 16:32, :].reshape(NREP * 16, LANES).astype(F32)
     for c in range(8):
         for t in range(2):
             piece = af[pl.ds(2 * c + t, NREP, stride=16), :]
             xs[t * NREP : (t + 1) * NREP, c * LANES : (c + 1) * LANES] = piece.astype(BF16)
     every = lax.dot_general(xs[...], dnv[...].reshape(ADP * RANK, 8 * LANES), NT, preferred_element_type=F32)
+    known = ai[pl.ds(0, NREP, stride=16), :].astype(I32)
+    lane32 = lax.broadcasted_iota(I32, (NREP, LANES), 1)
+    own = ((known == me) & (lane32 < ROWS)).astype(I32)
+    within = jnp.where(pltpu.roll(own, 2 * ROWS, 1) > 0, known, 0)
+    within = jnp.sum(within.astype(F32), axis=-1, keepdims=True).astype(I32)
+    pick = jnp.concatenate([within, within], axis=0)
+    block = lax.broadcasted_iota(I32, (2 * NREP, ADP * RANK), 1) // RANK
+    chosen = block == pick
     every = jnp.where(chosen, every, 0.0)
     folded = every[:, :LANES]
     for v in range(1, 8):
@@ -212,35 +230,39 @@
 
     def to_tp(d):
         pltpu.make_async_remote_copy(
-            tb, trec.at[tp], send_sem.at[6], recv_sem.at[6], device_id=(me, d), device_id_type=MESH
+            tb, trec.at[tp], send_sem.at[2], recv_sem.at[2], device_id=(me, d), device_id_type=MESH
         ).start()
 
     tp_peers(to_tp)
-    pltpu.make_async_copy(tb, trec.at[tp], recv_sem.at[6]).start()
-
-    target = known // SLOTS
+    pltpu.make_async_copy(tb, trec.at[tp], recv_sem.at[2]).start()
+
+    pltpu.make_async_copy(mrec, mrec, recv_sem.at[4]).wait()
+    named = mrec[:, 0, :]
+    target = named // SLOTS
     rank = jnp.zeros((NREP, LANES), I32)
     for back in range(1, ROWS):
-        same = (pltpu.roll(target, back, 1) == target) & (lane32 >= ROWS + back)
+        same = (pltpu.roll(target, back, 1) == target) & (lane32 >= back)
         rank = rank + same.astype(I32)
     code = lax.broadcasted_iota(I32, (NREP, LANES), 0) * 2 + rank
-    serving = (lane32 >= ROWS) & (lane32 < 2 * ROWS)
     for n in range(ROWS):
-        hit = serving & (known == me * SLOTS + ROWS + n)
+        hit = (lane32 < ROWS) & (named == me * SLOTS + ROWS + n)
         code_s[n] = jnp.max(jnp.where(hit, code, -1))
-        line_s[n] = jnp.max(jnp.where(hit, lane32 - ROWS, 0))
-
-    goal = jnp.sum(jnp.where(pltpu.roll(own.astype(I32), ROWS, 1) > 0, known, 0).astype(F32), axis=-1, keepdims=True)
+        line_s[n] = jnp.max(jnp.where(hit, lane32, 0))
+
+    slot = known * SLOTS + pltpu.roll(known, LANES - 2 * ROWS, 1)
+    goal = jnp.sum(jnp.where(pltpu.roll(own, ROWS, 1) > 0, slot, 0).astype(F32), axis=-1, keepdims=True)
     held = jnp.sum(own.astype(F32), axis=-1, keepdims=True)
     goal = jnp.where(held > 0.0, goal, -1.0)
     goal = jnp.broadcast_to(jnp.concatenate([goal, goal], axis=0), (2 * NREP, LANES)).T[0:1, :]
-    line = lax.broadcasted_iota(I32, (NREP * 16, 2 * NREP), 0)
-    from_token = lax.broadcasted_iota(I32, (NREP * 16, 2 * NREP), 1) // NREP
-    wanted = (line // 16) * SLOTS + ROWS + (line % 16) // 2
-    route[...] = jnp.where((goal == wanted.astype(F32)) & (from_token == line % 2), 1.0, 0.0).astype(BF16)
-
-    received(trec, 6)
-    l_up.wait()
+    line = lax.broadcasted_iota(I32, (NREP * 32, 2 * NREP), 0)
+    column = lax.broadcasted_iota(I32, (NREP * 32, 2 * NREP), 1)
+    to, part = line // 32, line % 32
+    for_slot = (part < 16) & (goal == (to * SLOTS + ROWS + part // 2).astype(F32))
+    for_own = (part >= 16) & (part < 18) & (column % NREP == to)
+    wanted = (for_slot | for_own) & (column // NREP == part % 2)
+    route[...] = jnp.where(wanted, 1.0, 0.0).astype(BF16)
+
+    pltpu.make_async_copy(trec, trec, recv_sem.at[2]).wait()
     low = trec[0]
     for n in range(1, TP):
         low = low + trec[n]
@@ -251,37 +273,32 @@
     )
     wide = jnp.where(chosen, jnp.concatenate([spread] * 8, axis=1), 0.0).astype(BF16)
     term = jnp.dot(wide, upv[...], preferred_element_type=F32)
-    cs[:, 0, :] = term[:NREP]
-    cs[:, 1, :] = term[NREP:]
-    spread_out = jnp.dot(route[...], term.astype(BF16), preferred_element_type=F32)
-    sb3[...] = spread_out.astype(BF16).reshape(NREP, 16, LANES)
-    exchange((lambda d: cs.at[d], crec, 3))
-    exchange((lambda d: sb3.at[d], mvrec, 5))
-
-    received(grec, 4)
-    received(wrec, 2)
+    sb3[...] = jnp.dot(route[...], term.astype(BF16), preferred_element_type=F32).astype(BF16).reshape(NREP, 32, LANES)
+    exchange(sb3, mvrec, 18, 3)
+
+    received(grec, 34, 1)
     for n in range(ROWS):
         safe = jnp.clip(code_s[n], 0, 2 * NREP - 1)
         shift = (LANES - jnp.clip(line_s[n], 0, ROWS - 1) * 16) % LANES
-        wq[2 * n : 2 * n + 2, :] = pltpu.roll(wrec[safe // 2], shift, 1)
+        wq[2 * n : 2 * n + 2, :] = pltpu.roll(grec[safe // 2, 32:48].astype(F32), shift, 1)[0:2]
     column = wq[...].T[0:16, :] * 0.5
     for n in range(ROWS):
         safe = jnp.clip(code_s[n], 0, 2 * NREP - 1)
-        base[n] = jnp.where(code_s[n] >= 0, grec[safe // 2, safe % 2].astype(F32), 0.0)
+        one, two = grec[safe // 2, 0:16].astype(F32), grec[safe // 2, 16:32].astype(F32)
+        base[n] = jnp.where(code_s[n] >= 0, jnp.where(safe % 2 == 1, two, one), 0.0)
         gain0[n] = jnp.broadcast_to(column[:, 2 * n : 2 * n + 1], (16, LANES))
         gain1[n] = jnp.broadcast_to(column[:, 2 * n + 1 : 2 * n + 2], (16, LANES))
-    received(crec, 3)
+    received(mvrec, 18, 3)
     for r in range(ROWS):
-        back = crec[owners[r]]
+        back = mvrec[owners[r], 16:32].astype(F32)
         value0 = (pvs[r : r + 1, :] + 0.5 * back[0:1]).astype(BF16).astype(F32)
         value1 = (pvs[ROWS + r : ROWS + r + 1, :] + 0.5 * back[1:2]).astype(BF16).astype(F32)
         done = (mixed[r] + wn0s[r] * value0 + wn1s[r] * value1).astype(BF16)
         kept = slots[r] == me * SLOTS + r
         out[r] = jnp.where(kept, done, jnp.zeros((16, LANES), BF16))
-    received(mvrec, 5)
-    extra = mvrec[0].astype(F32)
+    extra = mvrec[0, 0:16].astype(F32)
     for n in range(1, NREP):
-        extra = extra + mvrec[n].astype(F32)
+        extra = extra + mvrec[n, 0:16].astype(F32)
     for n in range(ROWS):
         added = gain0[n] * extra[2 * n : 2 * n + 1] + gain1[n] * extra[2 * n + 1 : 2 * n + 2]
         out[ROWS + n] = (base[n] + added).astype(BF16)
@@ -289,13 +306,12 @@
     def sent(ref, n):
         pltpu.make_async_copy(ref, ref, send_sem.at[n]).wait()
 
-    sent(sb.at[pl.ds(0, NREP - 1)], 0)
-    sent(mrec.at[pl.ds(0, NREP - 1)], 1)
-    sent(trec.at[pl.ds(0, TP - 1)], 6)
-    sent(wrec.at[pl.ds(0, NREP - 1)], 2)
-    sent(cs.at[pl.ds(0, NREP - 1)], 3)
-    sent(sb4.at[pl.ds(0, NREP - 1)], 4)
-    sent(sb3.at[pl.ds(0, NREP - 1)], 5)
+    others = pl.ds(0, NREP - 1)
+    sent(sb.at[others, pl.ds(0, 18)], 0)
+    sent(mrec.at[others], 4)
+    sent(sb4.at[others, pl.ds(0, 34)], 1)
+    sent(trec.at[pl.ds(0, TP - 1)], 2)
+    sent(sb3.at[others, pl.ds(0, 18)], 3)
 
 
 def shards(hidden, queries, wk, wv, down, up, ridx, home, table, lengths, serve, kc, vc):
@@ -309,19 +325,18 @@
         vmem((ADP, RANK, 1024), BF16), vmem((ADP * RANK, LANES), BF16), vmem((64, LANES, LANES), BF16), vmem((64, LANES, LANES), BF16),
         smem((8,), I32), smem((512,), I32), smem((8, 8), I32), smem((1, 8), I32), smem((8,), I32),
         vmem((ROWS * LANES, LANES), F32), vmem((16, 8192), BF16),
-        vmem((NREP, 16, LANES), BF16), vmem((NREP, 16, LANES), BF16),
-        vmem((NREP * 16, LANES), F32), vmem((2 * NREP, 1024), BF16),
+        vmem((NREP, 32, LANES), BF16), vmem((NREP, 32, LANES), BF16),
+        vmem((NREP * 16, LANES), F32), vmem((NREP * 16, LANES), F32), vmem((2 * NREP, 1024), BF16),
         vmem((1, LANES), I32), vmem((NREP, 1, LANES), I32),
         vmem((NREP, LANES), F32), vmem((TP, NREP, LANES), F32),
-        vmem((NREP, 2, LANES), F32), vmem((NREP, 2, LANES), F32),
         vmem((ROWS, 16, LANES), F32), vmem((ROWS, 16, LANES), F32), vmem((ROWS, 16, LANES), F32),
         vmem((16, LANES), F32), vmem((16, LANES), F32),
-        vmem((ROWS, 16, LANES), BF16), vmem((ROWS, 16, LANES), F32), vmem((2, LANES), F32), vmem((NREP, 2, LANES), F32),
-        vmem((NREP, 2, 16, LANES), BF16), vmem((NREP, 2, 16, LANES), BF16),
-        vmem((NREP * 16, 2 * NREP), BF16), vmem((NREP, 16, LANES), BF16), vmem((NREP, 16, LANES), BF16),
+        vmem((ROWS, 16, LANES), BF16), vmem((ROWS, 16, LANES), F32),
+        vmem((NREP, 48, LANES), BF16), vmem((NREP, 48, LANES), BF16),
+        vmem((NREP * 32, 2 * NREP), BF16), vmem((NREP, 32, LANES), BF16), vmem((NREP, 32, LANES), BF16),
         vmem((ROWS, 16, LANES), F32), vmem((ROWS, 16, LANES), F32), vmem((ROWS, 16, LANES), F32),
         vmem((8, LANES), I32), smem((8, LANES), I32), smem((ROWS,), I32), smem((ROWS,), I32), vmem((16, LANES), F32),
-        pltpu.SemaphoreType.DMA((14,)), pltpu.SemaphoreType.DMA((7,)), pltpu.SemaphoreType.DMA((7,)),
+        pltpu.SemaphoreType.DMA((14,)), pltpu.SemaphoreType.DMA((5,)), pltpu.SemaphoreType.DMA((5,)),
     ]
     hid, qin, wk, wv, dn, upr, ridx, home, table, lengths, serve, kc, vc = (pltpu.with_memory_space_constraint(a, pltpu.HBM) for a in (hid, qin, wk, wv, dn, upr, ridx, home, table, lengths, serve, kc, vc))
     result = pl.pallas_call(

time: 31.4 us -> 30.3 us (0.965)
  Pallas kernels: 30.7 us -> 29.6 us
    pallas_call x1, Pallas kernels: 30.7 us -> 29.6 us  [shards(): pl.pallas_call(kernel, out_shape=jax.ShapeDtypeStruct((SLOTS, 16, LANES),...]
where the time goes in v5:
time: 30.3 us; the launch traced here: 30.2 us
  Pallas kernels  29.6 us (98%)
  local copies, waits for them, and re-layouts  0.63 us (2%)
    pallas_call x1, Pallas kernels, shards(): pl.pallas_call(kernel, out_shape=jax.ShapeDtypeStruct((SLOTS, 16, LANES),...  29.6 us
    unnamed x1, local copies, waits for them, and re-layouts  0.63 us

profile of v5, /device:TPU:1, one launch (start us, length us, event | category | flops | bytes accessed | tf_op | source)
XLA Modules:
  0.0 30.2 jit_solution(9251125975072146433)
XLA Ops:
  0.0 29.6 %decode.1 = bf16[16,16,128]{2,1,0:T(8,128)(2,1)S(1)} custom-call(bf16[8,128,128]{2,1,0:T(8,128)(2,1)} %bitcast.19, bf16[8,16,128]{2,1,0:T(8,128)(2,1)} %bitcast.21, bf16[8192,128]{1,0:T(8,128)(2,1)} %wk.1, bf16[8192,128]{1,0:T(8,128)(2,1)} %wv.1, bf16[16,64,1024]{2,1,0:T(8,128)(2,1)} %bitcast.18, bf16[1024,128]{1,0:T(8,128)(2,1)} %bitcast.20, s32[8]{0:T(128)} %ridx.1, ...), custom_call_target="tpu_custom_call" | custom-call | tf_op jit(solution)/shard_map/decode/pallas_call | solution.py:342
  29.6 0.6 %copy.18 = bf16[16,2,1024]{2,1,0:T(2,128)(2,1)} copy(bf16[16,2,1024]{2,1,0:T(2,128)(2,1)S(1)} %bitcast.17) | data formatting | bytes 131072

commit v6 on v5

--- a/solution.py
+++ b/solution.py
@@ -256,7 +256,8 @@
     goal = jnp.broadcast_to(jnp.concatenate([goal, goal], axis=0), (2 * NREP, LANES)).T[0:1, :]
     line = lax.broadcasted_iota(I32, (NREP * 32, 2 * NREP), 0)
     column = lax.broadcasted_iota(I32, (NREP * 32, 2 * NREP), 1)
-    to, part = line // 32, line % 32
+    to = ((mx + line // 256) % NX) * NZ + (mz + (line // 32) % NZ) % NZ
+    part = line % 32
     for_slot = (part < 16) & (goal == (to * SLOTS + ROWS + part // 2).astype(F32))
     for_own = (part >= 16) & (part < 18) & (column % NREP == to)
     wanted = (for_slot | for_own) & (column // NREP == part % 2)
@@ -273,8 +274,21 @@
     )
     wide = jnp.where(chosen, jnp.concatenate([spread] * 8, axis=1), 0.0).astype(BF16)
     term = jnp.dot(wide, upv[...], preferred_element_type=F32)
-    sb3[...] = jnp.dot(route[...], term.astype(BF16), preferred_element_type=F32).astype(BF16).reshape(NREP, 32, LANES)
-    exchange(sb3, mvrec, 18, 3)
+    term = term.astype(BF16)
+    head = pl.ds(0, 18)
+    for dx in (2, 1, 3, 0):
+        lines = pl.ds(dx * NZ * 32, NZ * 32)
+        routed = jnp.dot(route[lines], term, preferred_element_type=F32)
+        sb3[dx * NZ : (dx + 1) * NZ] = routed.astype(BF16).reshape(NZ, 32, LANES)
+        for dz in (4, 3, 5, 2, 6, 1, 7, 0):
+            part_of = sb3.at[dx * NZ + dz, head]
+            if dx or dz:
+                pltpu.make_async_remote_copy(
+                    part_of, mvrec.at[me, head], send_sem.at[3], recv_sem.at[3], device_id=(to_x[dx] + to_z[dz], tp),
+                    device_id_type=MESH,
+                ).start()
+            else:
+                pltpu.make_async_copy(part_of, mvrec.at[me, head], recv_sem.at[3]).start()
 
     received(grec, 34, 1)
     for n in range(ROWS):

time: 30.3 us -> 29.8 us (0.983)
  Pallas kernels: 29.6 us -> 29.1 us
    pallas_call x1, Pallas kernels: 29.6 us -> 29.1 us  [shards(): pl.pallas_call(kernel, out_shape=jax.ShapeDtypeStruct((SLOTS, 16, LANES),...]
where the time goes in v6:
time: 29.8 us
  Pallas kernels  29.1 us (98%)
  local copies, waits for them, and re-layouts  0.63 us (2%)
    pallas_call x1, Pallas kernels, shards(): pl.pallas_call(kernel, out_shape=jax.ShapeDtypeStruct((SLOTS, 16, LANES),...  29.1 us
    unnamed x1, local copies, waits for them, and re-layouts  0.63 us

profile of v6, /device:TPU:1, one launch (start us, length us, event | category | flops | bytes accessed | tf_op | source)
XLA Modules:
  0.0 29.8 jit_solution(4724783262596418265)
XLA Ops:
  0.0 29.1 %decode.1 = bf16[16,16,128]{2,1,0:T(8,128)(2,1)S(1)} custom-call(bf16[8,128,128]{2,1,0:T(8,128)(2,1)} %bitcast.19, bf16[8,16,128]{2,1,0:T(8,128)(2,1)} %bitcast.21, bf16[8192,128]{1,0:T(8,128)(2,1)} %wk.1, bf16[8192,128]{1,0:T(8,128)(2,1)} %wv.1, bf16[16,64,1024]{2,1,0:T(8,128)(2,1)} %bitcast.18, bf16[1024,128]{1,0:T(8,128)(2,1)} %bitcast.20, s32[8]{0:T(128)} %ridx.1, ...), custom_call_target="tpu_custom_call" | custom-call | tf_op jit(solution)/shard_map/decode/pallas_call | solution.py:356
  29.1 0.6 %copy.18 = bf16[16,2,1024]{2,1,0:T(2,128)(2,1)} copy(bf16[16,2,1024]{2,1,0:T(2,128)(2,1)S(1)} %bitcast.17) | data formatting | bytes 131072

commit v7 on v6

--- a/solution.py
+++ b/solution.py
@@ -20,7 +20,7 @@
 LOG_BASE = math.log(1000000.0)
 FAR_FIRST = sorted(
     [(x, z) for x in range(NX) for z in range(NZ) if x or z],
-    key=lambda o: -(min(o[0], NX - o[0]) + min(o[1], NZ - o[1])),
+    key=lambda o: (-min(o[1], NZ - o[1]), -min(o[0], NX - o[0])),
 )
 
 

time: 29.8 us -> 29.4 us (0.987)
  Pallas kernels: 29.1 us -> 28.7 us
    pallas_call x1, Pallas kernels: 29.1 us -> 28.7 us  [shards(): pl.pallas_call(kernel, out_shape=jax.ShapeDtypeStruct((SLOTS, 16, LANES),...]
where the time goes in v7:
time: 29.4 us; the launch traced here: 29.3 us
  Pallas kernels  28.7 us (98%)
  local copies, waits for them, and re-layouts  0.63 us (2%)
    pallas_call x1, Pallas kernels, shards(): pl.pallas_call(kernel, out_shape=jax.ShapeDtypeStruct((SLOTS, 16, LANES),...  28.7 us
    unnamed x1, local copies, waits for them, and re-layouts  0.63 us

profile of v7, /device:TPU:1, one launch (start us, length us, event | category | flops | bytes accessed | tf_op | source)
XLA Modules:
  0.0 29.3 jit_solution(17759382062914665424)
XLA Ops:
  0.0 28.7 %decode.1 = bf16[16,16,128]{2,1,0:T(8,128)(2,1)S(1)} custom-call(bf16[8,128,128]{2,1,0:T(8,128)(2,1)} %bitcast.19, bf16[8,16,128]{2,1,0:T(8,128)(2,1)} %bitcast.21, bf16[8192,128]{1,0:T(8,128)(2,1)} %wk.1, bf16[8192,128]{1,0:T(8,128)(2,1)} %wv.1, bf16[16,64,1024]{2,1,0:T(8,128)(2,1)} %bitcast.18, bf16[1024,128]{1,0:T(8,128)(2,1)} %bitcast.20, s32[8]{0:T(128)} %ridx.1, ...), custom_call_target="tpu_custom_call" | custom-call | tf_op jit(solution)/shard_map/decode/pallas_call | solution.py:356
  28.7 0.6 %copy.18 = bf16[16,2,1024]{2,1,0:T(2,128)(2,1)} copy(bf16[16,2,1024]{2,1,0:T(2,128)(2,1)S(1)} %bitcast.17) | data formatting | bytes 131072

commit v8 on v7

--- a/solution.py
+++ b/solution.py
@@ -212,7 +212,6 @@
         for t in range(2):
             piece = af[pl.ds(2 * c + t, NREP, stride=16), :]
             xs[t * NREP : (t + 1) * NREP, c * LANES : (c + 1) * LANES] = piece.astype(BF16)
-    every = lax.dot_general(xs[...], dnv[...].reshape(ADP * RANK, 8 * LANES), NT, preferred_element_type=F32)
     known = ai[pl.ds(0, NREP, stride=16), :].astype(I32)
     lane32 = lax.broadcasted_iota(I32, (NREP, LANES), 1)
     own = ((known == me) & (lane32 < ROWS)).astype(I32)
@@ -221,10 +220,12 @@
     pick = jnp.concatenate([within, within], axis=0)
     block = lax.broadcasted_iota(I32, (2 * NREP, ADP * RANK), 1) // RANK
     chosen = block == pick
-    every = jnp.where(chosen, every, 0.0)
-    folded = every[:, :LANES]
-    for v in range(1, 8):
-        folded = folded + every[:, v * LANES : (v + 1) * LANES]
+    folded = jnp.zeros((2 * NREP, LANES), F32)
+    for g in range(4):
+        some = dnv[4 * g : 4 * g + 4].reshape(4 * RANK, 8 * LANES)
+        some = lax.dot_general(xs[...], some, NT, preferred_element_type=F32)
+        some = jnp.where(chosen[:, g * 4 * RANK : (g + 1) * 4 * RANK], some, 0.0)
+        folded = folded + some[:, :LANES] + some[:, LANES:]
     folded = folded + pltpu.roll(folded, RANK, 1)
     tb[...] = jnp.where(lane32 < RANK, folded[:NREP], folded[NREP:])
 
@@ -272,8 +273,12 @@
     spread = jnp.concatenate(
         [jnp.where(lane32 < RANK, low, other), jnp.where(lane32 < RANK, other, low)], axis=0
     )
-    wide = jnp.where(chosen, jnp.concatenate([spread] * 8, axis=1), 0.0).astype(BF16)
-    term = jnp.dot(wide, upv[...], preferred_element_type=F32)
+    both = jnp.concatenate([spread] * 2, axis=1)
+    term = jnp.zeros((2 * NREP, LANES), F32)
+    for g in range(4):
+        lines = slice(g * 4 * RANK, (g + 1) * 4 * RANK)
+        wide = jnp.where(chosen[:, lines], both, 0.0).astype(BF16)
+        term = term + jnp.dot(wide, upv[lines, :], preferred_element_type=F32)
     term = term.astype(BF16)
     head = pl.ds(0, 18)
     for dx in (2, 1, 3, 0):

time: 29.4 us -> 29.4 us (level)
  no operation moved by 1% of the time
where the time goes in v8:
time: 29.4 us; the launch traced here: 29.3 us
  Pallas kernels  28.7 us (98%)
  local copies, waits for them, and re-layouts  0.63 us (2%)
    pallas_call x1, Pallas kernels, shards(): pl.pallas_call(kernel, out_shape=jax.ShapeDtypeStruct((SLOTS, 16, LANES),...  28.7 us
    unnamed x1, local copies, waits for them, and re-layouts  0.63 us

profile of v8, /device:TPU:1, one launch (start us, length us, event | category | flops | bytes accessed | tf_op | source)
XLA Modules:
  0.0 29.3 jit_solution(16467818338540261078)
XLA Ops:
  0.0 28.7 %decode.1 = bf16[16,16,128]{2,1,0:T(8,128)(2,1)S(1)} custom-call(bf16[8,128,128]{2,1,0:T(8,128)(2,1)} %bitcast.19, bf16[8,16,128]{2,1,0:T(8,128)(2,1)} %bitcast.21, bf16[8192,128]{1,0:T(8,128)(2,1)} %wk.1, bf16[8192,128]{1,0:T(8,128)(2,1)} %wv.1, bf16[16,64,1024]{2,1,0:T(8,128)(2,1)} %bitcast.18, bf16[1024,128]{1,0:T(8,128)(2,1)} %bitcast.20, s32[8]{0:T(128)} %ridx.1, ...), custom_call_target="tpu_custom_call" | custom-call | tf_op jit(solution)/shard_map/decode/pallas_call | solution.py:361
  28.7 0.6 %copy.18 = bf16[16,2,1024]{2,1,0:T(2,128)(2,1)} copy(bf16[16,2,1024]{2,1,0:T(2,128)(2,1)S(1)} %bitcast.17) | data formatting | bytes 131072
